TPU v7x, 32 devices: a whole 2x2x4 slice. The times are simulated.
32 devices in a mesh: ev: 16 (over z, y, core), st: 2 (over x).
Axes of the slice: x: 2, y: 2, z: 4, core: 2. Of those that a mesh axis runs over, the one named last changes fastest.
Arguments:
- strain: bfloat16 [2, 6, 256, 4096], P(None, None, 'ev'), may hold values from -0.068359375 to 0.068359375
- green: bfloat16 [2, 3, 256, 6, 4096], P(None, None, 'st', None, 'ev'), may hold values from -6 to 6
- weights: bfloat16 [2, 3, 256, 256], P(None, None, 'ev', 'st'), may hold values from -0.15625 to 0.15625
- mask: int32 [256, 256], P('ev', 'st'), may hold values 0 or 1
Outputs:
- kernels: float32 [2, 4096], P(None, ('ev', 'st'))
All inputs are finite; a program needn't handle non-finite values. No bound on the sum of `mask` on one device may be relied on, other than what follows from the above.
Results may differ from a plain program's by a relative error of at most 0.0003.
Values may be sent and summed in bfloat16 or wider, within the bound.
No kernel may reach another device: no remote copies, remote signals or barrier semaphores. Data moves between devices by JAX's collectives and lax.ppermute only.
A program may use at most 128 MiB of HBM per device.

v0:
```python
import jax
import jax.numpy as jnp
from jax import lax
from jax.sharding import PartitionSpec as P


def local(strain, green, weights, mask):
    masked = weights * mask.astype(jnp.bfloat16)[None, None]
    cells_dev = green.shape[4]
    station_count = green.shape[2]
    event_rows = strain.shape[2]
    ev_count = lax.axis_size("ev")
    st_count = lax.axis_size("st")
    sub_cells = cells_dev // st_count
    shaped = strain.reshape(2, 6, event_rows, ev_count, st_count, sub_cells)
    selected = lax.dynamic_index_in_dim(shaped, lax.axis_index("st"), 4, keepdims=False)
    selected = selected.reshape(2, 6, event_rows, ev_count * sub_cells)
    narrow = lax.all_to_all(selected, "ev", split_axis=3, concat_axis=2, tiled=True)
    strain_all = lax.all_gather(narrow, "st", axis=3, tiled=True)
    green_flat = green.reshape(2, 3, station_count, 6 * cells_dev)
    voigt = jnp.array([1.0, 1.0, 1.0, 2.0, 2.0, 2.0], jnp.float32)
    weight_rows = lax.all_gather(masked, "ev", axis=2, tiled=True)
    row_count = weight_rows.shape[2]
    products = jnp.einsum(
        "rfps,qfsn->rqpn", weight_rows, green_flat, preferred_element_type=jnp.float32
    )
    held_real = (products[0, 0] - products[1, 1]).reshape(row_count, 6, cells_dev)
    held_imag = (products[0, 1] + products[1, 0]).reshape(row_count, 6, cells_dev)
    strain_rows = strain_all.astype(jnp.float32)
    strain_real = jnp.swapaxes(strain_rows[0], 0, 1)
    strain_imag = jnp.swapaxes(strain_rows[1], 0, 1)
    trace_term = jnp.sum(
        strain_real[:, :3].sum(1) * held_real[:, :3].sum(1)
        - strain_imag[:, :3].sum(1) * held_imag[:, :3].sum(1),
        axis=0,
    )
    shear_term = jnp.sum(
        (strain_real * held_real - strain_imag * held_imag) * voigt[None, :, None], axis=(0, 1)
    )
    partial_value = jnp.stack([trace_term, shear_term])
    return lax.psum_scatter(partial_value, "st", scatter_dimension=1, tiled=True)


def solution(mesh):
    placed = (
        P(None, None, "ev", None),
        P(None, None, "st", None, "ev"),
        P(None, None, "ev", "st"),
        P("ev", "st"),
    )
    return jax.shard_map(
        local, mesh=mesh, in_specs=placed, out_specs=P(None, ("ev", "st")), check_vma=False
    )
```

profile of v0, /device:TPU:0, one launch (start us, length us, event | category | flops | bytes accessed | tf_op | source)
XLA Modules:
  0.0 143.1 jit_solution(11234989107015068082)
XLA Ops:
  6.5 2.8 %reshape.20 = bf16[2,6,16,16,2,128]{5,4,3,2,1,0:T(2,128)(2,1)S(1)} reshape(bf16[2,6,16,4096]{3,2,1,0:T(8,128)(2,1)} %param.5) | data formatting | bytes 3145728 | tf_op jit(solution)/shard_map/reshape | solution.py:15
  9.4 1.9 %constant_dynamic-slice_fusion = bf16[2,6,16,16,1,128]{5,4,3,2,1,0:T(2,128)(2,1)S(1)} fusion(bf16[2,6,16,16,2,128]{5,4,3,2,1,0:T(2,128)(2,1)S(1)} %reshape.20, s32[]{:T(128)S(6)} %select_n.4), kind=kLoop, calls=%fused_computation.14 | loop fusion | bytes 1572868 | tf_op jit(solution)/shard_map/jit(dynamic_index_in_dim)/dynamic_slice | solution.py:16
  11.3 11.5 %copy.44 = bf16[2,6,16,16,1,128]{2,0,1,5,3,4:T(2,128)(2,1)} copy(bf16[2,6,16,16,1,128]{5,4,3,2,1,0:T(2,128)(2,1)S(1)} %constant_dynamic-slice_fusion) | data formatting | bytes 1572864 | tf_op jit(solution)/shard_map/reshape | solution.py:17
  22.8 18.4 %reshape.28 = bf16[16,2,12288]{2,1,0:T(2,128)(2,1)} reshape(bf16[2048,6,2,16]{3,2,1,0:T(2,128)(2,1)} %bitcast.43) | data formatting | bytes 1572864
  41.2 7.5 %all-to-all-start = ((bf16[16,2,12288]{2,1,0:T(2,128)(2,1)}), bf16[16,2,12288]{2,1,0:T(2,128)(2,1)S(1)}, u32[]{:S(2)}, u32[]{:S(2)}) async-start(bf16[16,2,12288]{2,1,0:T(2,128)(2,1)} %reshape.28), calls=%async_computation | async-start | bytes 1572864 | tf_op jit(solution)/shard_map/all_to_all | solution.py:18
  48.8 3.1 %copy.33 = bf16[2,3,128,6,256]{2,4,3,1,0:T(8,128)(2,1)S(1)} copy(bf16[2,3,128,6,256]{4,2,3,1,0:T(8,128)(2,1)} %param.6) | data formatting | bytes 4718592 | tf_op args[1]
  51.9 15.5 %all-to-all-done = bf16[16,2,12288]{2,1,0:T(2,128)(2,1)S(1)} async-done(((bf16[16,2,12288]{2,1,0:T(2,128)(2,1)}), bf16[16,2,12288]{2,1,0:T(2,128)(2,1)S(1)}, u32[]{:S(2)}, u32[]{:S(2)}) %all-to-all-start) | async-done | bytes 786464 | tf_op jit(solution)/shard_map/all_to_all | solution.py:18
  67.4 5.6 %reshape.29 = bf16[2048,6,2,16]{3,2,1,0:T(2,128)(2,1)} reshape(bf16[16,2,12288]{2,1,0:T(2,128)(2,1)S(1)} %all-to-all-done) | data formatting | bytes 1572864
  73.0 14.8 %copy.46 = bf16[2,6,16,16,128]{4,2,3,1,0:T(8,128)(2,1)} copy(bf16[2,6,16,16,128]{2,0,1,4,3:T(2,128)(2,1)} %bitcast.42) | data formatting | bytes 1572864 | tf_op jit(solution)/shard_map/all_to_all | solution.py:18
  88.0 22.4 %all_gather.7 = bf16[2,3,256,128]{3,2,1,0:T(8,128)(2,1)S(1)} all-gather(bf16[2,3,16,128]{3,2,1,0:T(8,128)(2,1)S(1)} %broadcast_multiply_fusion), channel_id=1, replica_groups=mesh['ev'=16,'st'=2] {'ev'}, dimensions={2}, use_global_device_ids=true | all-gather | bytes 417792 | tf_op jit(solution)/shard_map/all_gather | solution.py:22
  110.4 1.8 %convolution_bitcast_fusion = f32[2,2,256,1536]{3,2,1,0:T(8,128)S(1)} fusion(bf16[2,3,128,1536,1]{2,3,1,0,4:T(8,128)(2,1)S(1)} %bitcast.48, bf16[2,3,256,128]{3,2,1,0:T(8,128)(2,1)S(1)} %all_gather.7), kind=kOutput, calls=%fused_computation | convolution fusion | flops 1207959552 | bytes 9043968 | tf_op jit(solution)/shard_map/rfps,qfsn->rqpn/dot_general | solution.py:24
  112.2 1.7 %slice_subtract_fusion = (f32[1,1,256,1536]{3,2,1,0:T(8,128)}, f32[1,1,256,1536]{3,2,1,0:T(8,128)S(1)}) fusion(f32[2,2,256,1536]{3,2,1,0:T(8,128)S(1)} %convolution_bitcast_fusion), kind=kLoop, calls=%fused_computation.3 | loop fusion | flops 786432 | bytes 9437184 | tf_op jit(solution)/shard_map/sub | solution.py:27
  113.9 1.9 %copy.35 = f32[1,1,256,1536]{2,3,1,0:T(8,128)S(1)} copy(f32[1,1,256,1536]{3,2,1,0:T(8,128)} %get-tuple-element.5) | data formatting | bytes 3145728 | tf_op jit(solution)/shard_map/sub | solution.py:27
  115.8 1.6 %copy.39 = f32[256,6,256]{2,0,1:T(8,128)} copy(f32[256,6,256]{0,2,1:T(8,128)S(1)} %bitcast.44) | data formatting | bytes 3145728 | tf_op jit(solution)/shard_map/sub | solution.py:27
  117.4 0.8 slice_reduce_fusion.2
  118.2 1.1 copy.36
  120.2 0.8 slice_reduce_fusion
  121.0 1.1 copy.38
  122.1 1.7 %convert_element_type.6 = f32[2,6,256,256]{3,2,1,0:T(8,128)S(1)} convert(bf16[2,6,256,256]{3,2,1,0:T(8,128)(2,1)} %all-gather.2.cloned.1.call-done) | non-fusion elementwise | flops 786432 | bytes 4718592 | tf_op jit(solution)/shard_map/convert_element_type | solution.py:29
  124.2 1.3 copy-done
  125.5 0.7 multiply_reduce_fusion
  126.2 0.8 copy.48
  127.0 7.8 %reduce-scatter.4.cloned.1.call-done = f32[128,2]{1,0:T(8,128)} async-done(((f32[256,2]{1,0:T(8,128)}), f32[128,2]{1,0:T(8,128)}) %reduce-scatter.4.cloned.1.call-update) | async-done | bytes 1040
  134.8 1.5 %copy.49 = f32[2,128]{1,0:T(2,128)} copy(f32[2,128]{0,1:T(8,128)} %bitcast.51) | data formatting | bytes 2048
  (20 shorter events, 1.5 us)
Async XLA Ops:
  41.2 7.6 %copy-start.2 = (s32[16,128]{1,0:T(8,128)S(1)}, s32[16,128]{1,0:T(8,128)}, u32[]{:S(2)}) copy-start(s32[16,128]{1,0:T(8,128)} %param.8) | copy-start | bytes 24580
  41.2 26.2 %all-to-all-start = ((bf16[16,2,12288]{2,1,0:T(2,128)(2,1)}), bf16[16,2,12288]{2,1,0:T(2,128)(2,1)S(1)}, u32[]{:S(2)}, u32[]{:S(2)}) async-start(bf16[16,2,12288]{2,1,0:T(2,128)(2,1)} %reshape.28), calls=%async_computation | async-start | bytes 1572864 | tf_op jit(solution)/shard_map/all_to_all | solution.py:18
  48.7 73.4 %all-gather.2.cloned.1.call-start = ((), (), s32[]{:S(2)}) async-start(), calls=%async_computation.2 | async-start | bytes 2359296 | tf_op jit(solution)/shard_map/all_gather | solution.py:19
  73.0 14.9 %copy-start.1 = (bf16[2,3,16,128]{3,2,1,0:T(8,128)(2,1)S(1)}, bf16[2,3,16,128]{3,2,1,0:T(8,128)(2,1)}, u32[]{:S(2)}) copy-start(bf16[2,3,16,128]{3,2,1,0:T(8,128)(2,1)} %param.7) | copy-start | bytes 73732
  87.9 46.9 %reduce-scatter.4.cloned.1.call-start = ((), (), s32[]{:S(2)}) async-start(), calls=%async_computation.3 | async-start | bytes 196608
  124.1 1.4 copy-start
  124.1 1.4 copy-start.3
Sparse Core Ops, SparseCore 0:
  88.0 27.8 all-gather.1
  127.1 7.6 reduce-scatter.3
where the time goes:
time: 144 us; the launch traced here: 143 us
  local copies, waits for them, and re-layouts  68.5 us (48%)
  waiting for transfers between devices  23.4 us (16%)
  blocking collectives  22.4 us (16%)
  between operations  13.6 us (9%)
  starting transfers between devices  7.63 us (5%)
  other arithmetic  5.83 us (4%)
  matrix products  1.83 us (1%)
    unnamed x13, local copies, waits for them, and re-layouts  30.6 us
    all_gather x1, blocking collectives, local(): weight_rows = lax.all_gather(masked, 'ev', axis=2, tiled=True)  22.4 us
    all_to_all x1, waiting for transfers between devices, local(): lax.all_to_all(selected, 'ev', split_axis=3, concat_axis=2, tiled=True)  15.5 us
    all_to_all x1, local copies, waits for them, and re-layouts, local(): lax.all_to_all(selected, 'ev', split_axis=3, concat_axis=2, tiled=True)  14.8 us
    reshape x1, local copies, waits for them, and re-layouts, local(): selected = selected.reshape(2, 6, event_rows, ev_count * sub_cells)  11.5 us
    unnamed x3, waiting for transfers between devices  7.81 us
    all_to_all x1, starting transfers between devices, local(): lax.all_to_all(selected, 'ev', split_axis=3, concat_axis=2, tiled=True)  7.55 us
    sub x2, local copies, waits for them, and re-layouts, local(): products[0, 0] - products[1, 1]  3.5 us
  transfers between devices with their start and end apart: 3, of which 2 were waited for; matrix products, arithmetic and copies ran while one was open for 10% of the time, Pallas kernels for 0%

commit v1 on v0

--- a/solution.py
+++ b/solution.py
@@ -1,10 +1,17 @@
+import functools
+
 import jax
 import jax.numpy as jnp
 from jax import lax
+from jax.experimental import pallas as pl
+from jax.experimental.pallas import tpu as pltpu
 from jax.sharding import PartitionSpec as P
 
-
-def local(strain, green, weights, mask):
+LANES = 128
+COMPONENTS = 6
+
+
+def general(strain, green, weights, mask):
     masked = weights * mask.astype(jnp.bfloat16)[None, None]
     cells_dev = green.shape[4]
     station_count = green.shape[2]
@@ -41,6 +48,338 @@
     return lax.psum_scatter(partial_value, "st", scatter_dimension=1, tiled=True)
 
 
+VMEM_LIMIT = 24 * 1024 * 1024
+GREEN_LIMIT = 64_700_000
+VMEM_ALL = 65_800_000
+
+
+def params(limit=VMEM_LIMIT):
+    return pltpu.CompilerParams(vmem_limit_bytes=limit)
+
+
+def in_vmem():
+    return pl.BlockSpec(memory_space=pltpu.VMEM)
+
+
+def in_smem():
+    return pl.BlockSpec(memory_space=pltpu.SMEM)
+
+
+def in_hbm():
+    return pl.BlockSpec(memory_space=pltpu.HBM)
+
+
+def green_copies(green_ref, buf, sems, first, lane):
+    triple = buf.shape[1]
+    return [
+        pltpu.make_async_copy(
+            green_ref.at[i, pl.ds(first, triple), :, pl.ds(lane, LANES)], buf.at[i], sems.at[i]
+        )
+        for i in range(buf.shape[0])
+    ]
+
+
+def first_kernel(
+    side_ref, green_ref, weights_ref, mask_ref,
+    sent_ref, masked_ref, buf, weights_buf, mask_buf, sems, small_sems, out_sem,
+):
+    lane = pl.multiple_of((1 - side_ref[0]) * LANES, LANES)
+    small = [
+        pltpu.make_async_copy(weights_ref, weights_buf, small_sems.at[0]),
+        pltpu.make_async_copy(mask_ref, mask_buf, small_sems.at[1]),
+    ]
+    copies = green_copies(green_ref, buf, sems, 0, lane)
+    for copy in small + copies:
+        copy.start()
+    for copy in small:
+        copy.wait()
+    keep = mask_buf[...].astype(jnp.bfloat16)
+    for r in range(2):
+        for f in range(3):
+            masked_ref[r, f] = weights_buf[r, f] * keep
+    for copy in copies:
+        copy.wait()
+    give = pltpu.make_async_copy(buf, sent_ref, out_sem)
+    give.start()
+    give.wait()
+
+
+def first_pieces(side, green, weights, mask):
+    rows, _, stations, _ = green.shape
+    shape = (rows, COMPONENTS // 2, stations, LANES)
+    return pl.pallas_call(
+        first_kernel,
+        out_shape=(
+            jax.ShapeDtypeStruct(shape, green.dtype),
+            jax.ShapeDtypeStruct(weights.shape, weights.dtype),
+        ),
+        in_specs=[in_smem(), in_hbm(), in_hbm(), in_hbm()],
+        out_specs=(in_hbm(), in_vmem()),
+        scratch_shapes=[
+            pltpu.VMEM(shape, green.dtype),
+            pltpu.VMEM(weights.shape, weights.dtype),
+            pltpu.VMEM(mask.shape, mask.dtype),
+            pltpu.SemaphoreType.DMA((rows,)),
+            pltpu.SemaphoreType.DMA((2,)),
+            pltpu.SemaphoreType.DMA,
+        ],
+        compiler_params=params(VMEM_ALL),
+        name="first_pieces",
+    )(side, green, weights, mask)
+
+
+def green_kernel(side_ref, green_ref, sent_ref, buf, sems, out_sem):
+    lane = pl.multiple_of((1 - side_ref[0]) * LANES, LANES)
+    copies = green_copies(green_ref, buf, sems, COMPONENTS // 2, lane)
+    for copy in copies:
+        copy.start()
+    for copy in copies:
+        copy.wait()
+    give = pltpu.make_async_copy(buf, sent_ref, out_sem)
+    give.start()
+    give.wait()
+
+
+def green_pieces(side, green):
+    rows, _, stations, _ = green.shape
+    shape = (rows, COMPONENTS // 2, stations, LANES)
+    return pl.pallas_call(
+        green_kernel,
+        out_shape=jax.ShapeDtypeStruct(shape, green.dtype),
+        in_specs=[in_smem(), in_hbm()],
+        out_specs=in_hbm(),
+        scratch_shapes=[
+            pltpu.VMEM(shape, green.dtype),
+            pltpu.SemaphoreType.DMA((rows,)),
+            pltpu.SemaphoreType.DMA,
+        ],
+        compiler_params=params(GREEN_LIMIT),
+        name="green_pieces",
+    )(side, green)
+
+
+def strain_kernel(st_count, side_ref, strain_ref, pieces_ref, buf, sems, out_sems):
+    count = pieces_ref.shape[0]
+    takes, gives = [], []
+    for i in range(count):
+        lane = pl.multiple_of((i * st_count + side_ref[0]) * LANES, LANES)
+        takes.append(
+            pltpu.make_async_copy(strain_ref.at[:, :, pl.ds(lane, LANES)], buf.at[i], sems.at[i])
+        )
+    groups = out_sems.shape[0]
+    size = count // groups
+    for g in range(groups):
+        part = pl.ds(g * size, size)
+        gives.append(pltpu.make_async_copy(buf.at[part], pieces_ref.at[part], out_sems.at[g]))
+    for copy in takes:
+        copy.start()
+    for g in range(groups):
+        for copy in takes[g * size : (g + 1) * size]:
+            copy.wait()
+        gives[g].start()
+    for copy in gives:
+        copy.wait()
+
+
+def strain_pieces(side, strain, ev_count, st_count):
+    parts, events, _ = strain.shape
+    shape = (ev_count, parts, events, LANES)
+    return pl.pallas_call(
+        functools.partial(strain_kernel, st_count),
+        out_shape=jax.ShapeDtypeStruct(shape, strain.dtype),
+        in_specs=[in_smem(), in_hbm()],
+        out_specs=in_hbm(),
+        scratch_shapes=[
+            pltpu.VMEM(shape, strain.dtype),
+            pltpu.SemaphoreType.DMA((ev_count,)),
+            pltpu.SemaphoreType.DMA((4,)),
+        ],
+        compiler_params=params(VMEM_ALL),
+        name="strain_pieces",
+    )(side, strain)
+
+
+def stacked(block_ref, components, lane=0):
+    columns = []
+    for c in components:
+        columns.append(
+            jnp.concatenate(
+                [block_ref[i, c, :, pl.ds(lane, LANES)] for i in range(block_ref.shape[0])], axis=0
+            )
+        )
+    return columns[0] if len(columns) == 1 else jnp.concatenate(columns, axis=1)
+
+
+def product(left, right):
+    return jnp.dot(left, right, preferred_element_type=jnp.float32)
+
+
+def held_kernel(me_ref, side_ref, near_ref, y_ref, core_ref, both_ref, green_ref, other_ref, held_ref, before_ref, lhs_ref):
+    quads = (near_ref, core_ref, y_ref, both_ref)
+    _, far, _, _, events, stations = near_ref.shape
+    count = len(quads) * far
+    half = count * events
+    for x in range(count):
+        z, bit, place = 0, count // 2, 0
+        while bit > 2:
+            z += ((x // bit) & 1) << place
+            bit, place = bit // 2, place + 1
+        w_ref = quads[x & 3]
+        start = pl.multiple_of((me_ref[0] ^ x) * events, events)
+        rows = pl.ds(start, events)
+        low = pl.ds(start + half, events)
+        for h in range(2):
+            for f in range(3):
+                real = w_ref[h, z, 0, f]
+                imag = w_ref[h, z, 1, f]
+                first = slice(f * stations, (f + 1) * stations)
+                second = slice((3 + f) * stations, (4 + f) * stations)
+                lhs_ref[h, rows, first] = real
+                lhs_ref[h, low, first] = imag
+                lhs_ref[h, rows, second] = -imag
+                lhs_ref[h, low, second] = real
+    lane = pl.multiple_of(side_ref[0] * LANES, LANES)
+    wide = 2 * LANES
+    held_ref[:, :wide] = product(lhs_ref[0], stacked(green_ref, (0, 1), lane)) + product(
+        lhs_ref[1], stacked(other_ref, (0, 1))
+    )
+    middle = product(lhs_ref[0], stacked(green_ref, (2, 3), lane))
+    held_ref[:, wide:] = middle[:, :LANES] + product(lhs_ref[1], stacked(other_ref, (2,)))
+    before_ref[:, :LANES] = middle[:, LANES:]
+    before_ref[:, LANES:] = product(lhs_ref[0], stacked(green_ref, (4, 5), lane))
+
+
+def held_first(me, side, near, y, core, both, green, other):
+    _, far, _, _, events, stations = near.shape
+    rows = 8 * far * events
+    return pl.pallas_call(
+        held_kernel,
+        out_shape=(
+            jax.ShapeDtypeStruct((rows, COMPONENTS // 2 * LANES), jnp.float32),
+            jax.ShapeDtypeStruct((rows, COMPONENTS // 2 * LANES), jnp.float32),
+            jax.ShapeDtypeStruct((2, rows, 6 * stations), jnp.bfloat16),
+        ),
+        in_specs=[in_smem(), in_smem()] + [in_vmem()] * 6,
+        out_specs=(in_vmem(),) * 3,
+        compiler_params=params(),
+        name="held_first",
+    )(me, side, near, y, core, both, green, other)
+
+
+def rest_kernel(lhs_ref, other_ref, before_ref, rest_ref):
+    rest_ref[:, :LANES] = before_ref[:, :LANES] + product(lhs_ref[1], stacked(other_ref, (0,)))
+    rest_ref[:, LANES:] = before_ref[:, LANES:] + product(lhs_ref[1], stacked(other_ref, (1, 2)))
+
+
+def held_rest(lhs, other, before):
+    return pl.pallas_call(
+        rest_kernel,
+        out_shape=jax.ShapeDtypeStruct(before.shape, before.dtype),
+        in_specs=[in_vmem()] * 3,
+        out_specs=in_vmem(),
+        compiler_params=params(),
+        name="held_rest",
+    )(lhs, other, before)
+
+
+def combine_kernel(strain_ref, first_ref, rest_ref, o_ref):
+    blocks, _, events, _ = strain_ref.shape
+    half = blocks * events
+    trace = jnp.zeros((events, LANES), jnp.float32)
+    normal = jnp.zeros((events, LANES), jnp.float32)
+    cross = jnp.zeros((events, LANES), jnp.float32)
+    for b in range(blocks):
+        rows = slice(b * events, (b + 1) * events)
+        low = slice(half + b * events, half + (b + 1) * events)
+        sums = None
+        for c in range(COMPONENTS):
+            held_ref = first_ref if c < 3 else rest_ref
+            lanes = slice((c % 3) * LANES, (c % 3 + 1) * LANES)
+            real = strain_ref[b, c].astype(jnp.float32)
+            imag = strain_ref[b, COMPONENTS + c].astype(jnp.float32)
+            held_real = held_ref[rows, lanes]
+            held_imag = held_ref[low, lanes]
+            term = real * held_real - imag * held_imag
+            if c < 3:
+                normal = normal + term
+                four = (real, imag, held_real, held_imag)
+                sums = four if sums is None else tuple(x + y for x, y in zip(sums, four))
+            else:
+                cross = cross + term
+        trace = trace + (sums[0] * sums[2] - sums[1] * sums[3])
+    shear = normal + 2.0 * cross
+    o_ref[0:1, :] = jnp.sum(trace, axis=0, keepdims=True)
+    o_ref[1:2, :] = jnp.sum(shear, axis=0, keepdims=True)
+
+
+def combine(strain, first, rest):
+    return pl.pallas_call(
+        combine_kernel,
+        out_shape=jax.ShapeDtypeStruct((2, LANES), jnp.float32),
+        in_specs=[in_vmem()] * 3,
+        out_specs=in_vmem(),
+        compiler_params=params(),
+        name="combine",
+    )(strain, first, rest)
+
+
+def paired(strain, green, weights, mask):
+    return paired_steps(strain, green, weights, mask)
+
+
+def paired_steps(strain, green, weights, mask):
+    ev_count = lax.axis_size("ev")
+    st_count = lax.axis_size("st")
+    event_rows = strain.shape[2]
+    station_count = green.shape[2]
+    me = lax.axis_index("ev").astype(jnp.int32)[None]
+    side = lax.axis_index("st").astype(jnp.int32)[None]
+
+    def hop(x, bit):
+        return lax.ppermute(x, "ev", [(i, i ^ bit) for i in range(ev_count)])
+
+    def swap(x):
+        return lax.ppermute(x, "st", [(0, 1), (1, 0)])
+
+    green = jnp.transpose(green, (0, 1, 3, 2, 4)).reshape(6, COMPONENTS, station_count, 2 * LANES)
+    sent_first, masked = first_pieces(side, green, weights, mask)
+    other_first = swap(sent_first)
+
+    gathered = masked[None]
+    bit = ev_count // 2
+    while bit > 2:
+        gathered = jnp.concatenate([gathered, hop(gathered, bit)])
+        bit //= 2
+
+    pieces = strain_pieces(side, strain.reshape(12, event_rows, -1), ev_count, st_count)
+    moved = lax.all_to_all(pieces, "ev", 0, 0, tiled=True)
+
+    near = jnp.stack([gathered, swap(gathered)])
+    sent_rest = green_pieces(side, green)
+    other_rest = swap(sent_rest)
+    y = hop(near, 2)
+    core = hop(near, 1)
+    both = hop(y, 1)
+
+    first, before, lhs = held_first(me, side, near, y, core, both, green, other_first)
+    rest = held_rest(lhs, other_rest, before)
+    return combine(moved, first, rest)
+
+
+def local(strain, green, weights, mask):
+    ev_count = lax.axis_size("ev")
+    st_count = lax.axis_size("st")
+    fits = (
+        st_count == 2
+        and ev_count >= 8
+        and ev_count & (ev_count - 1) == 0
+        and green.shape[4] == st_count * LANES
+        and green.shape[2] % LANES == 0
+        and strain.shape[2] % 16 == 0
+    )
+    return (paired if fits else general)(strain, green, weights, mask)
+
+
 def solution(mesh):
     placed = (
         P(None, None, "ev", None),

time: 144 us -> 67.5 us (0.47)
  local copies, waits for them, and re-layouts: 68.5 us -> 1.67 us
  blocking collectives: 22.4 us -> 0 us
  waiting for transfers between devices: 23.4 us -> 37.6 us
  between operations: 13.6 us -> 0.07 us
  Pallas kernels: 0 us -> 10.5 us
  starting transfers between devices: 7.63 us -> 15.5 us
  other arithmetic: 5.83 us -> 1.52 us
  matrix products: 1.83 us -> 0 us
    ppermute x0 -> x8, waiting for transfers between devices: none -> 37.6 us  [the longest x5 26.1 us: hop(): return lax.ppermute(x, 'ev', [(i, i ^ bit) for i in range(ev_count)])]
    unnamed x13 -> x2, local copies, waits for them, and re-layouts: 30.6 us -> 1.67 us
    all_gather x1 -> x0, blocking collectives: 22.4 us -> none  [local(): weight_rows = lax.all_gather(masked, 'ev', axis=2, tiled=True)]
    all_to_all x1, waiting for transfers between devices: 15.5 us -> 0.01 us  [paired_steps(): moved = lax.all_to_all(pieces, 'ev', 0, 0, tiled=True)]
    all_to_all x1 -> x0, local copies, waits for them, and re-layouts: 14.8 us -> none  [local(): lax.all_to_all(selected, 'ev', split_axis=3, concat_axis=2, tiled=True)]
    reshape x2 -> x0, local copies, waits for them, and re-layouts: 14.4 us -> none  [the longest x1 11.5 us: local(): selected = selected.reshape(2, 6, event_rows, ev_count * sub_cells)]
    pallas_call x0 -> x6, Pallas kernels: none -> 10.5 us  [the longest x1 2.68 us: first_pieces(): pl.pallas_call(first_kernel, out_shape=(jax.ShapeDtypeStruct(shape, green...]
    ppermute x0 -> x8, starting transfers between devices: none -> 8.07 us  [the longest x5 4.42 us: hop(): return lax.ppermute(x, 'ev', [(i, i ^ bit) for i in range(ev_count)])]
  transfers between devices with their start and end apart: 3 -> 9, of which waited for: 2 -> 7; matrix products, arithmetic and copies ran while one was open for 10% -> 2% of each run, Pallas kernels for 0% -> 12%
where the time goes in v1:
time: 67.5 us; the launch traced here: 66.9 us
  waiting for transfers between devices  37.6 us (56%)
  starting transfers between devices  15.5 us (23%)
  Pallas kernels  10.5 us (16%)
  local copies, waits for them, and re-layouts  1.67 us (2%)
  other arithmetic  1.52 us (2%)
    ppermute x5, waiting for transfers between devices, hop(): return lax.ppermute(x, 'ev', [(i, i ^ bit) for i in range(ev_count)])  26.1 us
    ppermute x3, waiting for transfers between devices, swap(): return lax.ppermute(x, 'st', [(0, 1), (1, 0)])  11.5 us
    all_to_all x1, starting transfers between devices, paired_steps(): moved = lax.all_to_all(pieces, 'ev', 0, 0, tiled=True)  7.43 us
    ppermute x5, starting transfers between devices, hop(): return lax.ppermute(x, 'ev', [(i, i ^ bit) for i in range(ev_count)])  4.42 us
    ppermute x3, starting transfers between devices, swap(): return lax.ppermute(x, 'st', [(0, 1), (1, 0)])  3.65 us
    pallas_call x1, Pallas kernels, first_pieces(): pl.pallas_call(first_kernel, out_shape=(jax.ShapeDtypeStruct(shape, green...  2.68 us
    pallas_call x1, Pallas kernels, held_first(): pl.pallas_call(held_kernel, out_shape=(jax.ShapeDtypeStruct((rows, COMPON...  2.47 us
    pallas_call x1, Pallas kernels, green_pieces(): pl.pallas_call(green_kernel, out_shape=jax.ShapeDtypeStruct(shape, green....  2.01 us
  transfers between devices with their start and end apart: 9, of which 7 were waited for; matrix products, arithmetic and copies ran while one was open for 2% of the time, Pallas kernels for 12%

profile of v1, /device:TPU:0, one launch (start us, length us, event | category | flops | bytes accessed | tf_op | source)
XLA Modules:
  0.0 66.9 jit_solution(12388387363449093517)
XLA Ops:
  0.0 2.0 %strain_pieces.1 = bf16[16,12,16,128]{3,2,1,0:T(8,128)(2,1)} custom-call(s32[1]{0:T(128)} %bitcast.side_ref, bf16[12,16,4096]{2,1,0:T(8,128)(2,1)} %bitcast.13), custom_call_target="tpu_custom_call" | custom-call | tf_op jit(solution)/shard_map/strain_pieces/pallas_call | solution.py:187
  2.0 7.4 %all-to-all-start = ((bf16[16,12,16,128]{3,2,1,0:T(8,128)(2,1)}), bf16[16,12,16,128]{3,2,1,0:T(8,128)(2,1)S(1)}, u32[]{:S(2)}, u32[]{:S(2)}) async-start(bf16[16,12,16,128]{3,2,1,0:T(8,128)(2,1)} %strain_pieces.1), calls=%async_computation | async-start | bytes 1572864 | tf_op jit(solution)/shard_map/all_to_all | solution.py:355
  9.4 2.7 %first_pieces.1 = (bf16[6,3,128,128]{3,2,1,0:T(8,128)(2,1)}, bf16[2,3,16,128]{3,2,1,0:T(8,128)(2,1)}) custom-call(s32[1]{0:T(128)} %bitcast.side_ref, bf16[6,6,128,256]{3,2,1,0:T(8,128)(2,1)} %bitcast.10, bf16[2,3,16,128]{3,2,1,0:T(8,128)(2,1)} %weights_ref.1, s32[16,128]{1,0:T(8,128)} %mask_ref.1), custom_call_target="tpu_custom_call" | custom-call | tf_op jit(solution)/shard_map/first_pieces/pallas_call | solution.py:110
  12.1 2.9 %collective-permute-start = (bf16[1,2,3,16,128]{4,3,2,1,0:T(8,128)(2,1)}, bf16[1,2,3,16,128]{4,3,2,1,0:T(8,128)(2,1)S(1)}, u32[]{:S(2)}, u32[]{:S(2)}) collective-permute-start(bf16[1,2,3,16,128]{4,3,2,1,0:T(8,128)(2,1)} %bitcast.14), channel_id=1, source_target_pairs={{0,16},{2,18},{4,20},{6,22},{8,24},{10,26},{12,28},{14,30},{16,0},... | collective-permute-start | bytes 73736 | tf_op jit(solution)/shard_map/ppermute | solution.py:339
  15.0 16.4 %collective-permute-done = bf16[1,2,3,16,128]{4,3,2,1,0:T(8,128)(2,1)S(1)} collective-permute-done((bf16[1,2,3,16,128]{4,3,2,1,0:T(8,128)(2,1)}, bf16[1,2,3,16,128]{4,3,2,1,0:T(8,128)(2,1)S(1)}, u32[]{:S(2)}, u32[]{:S(2)}) %collective-permute-start) | collective-permute-done | bytes 24608 | tf_op jit(solution)/shard_map/ppermute | solution.py:339
  31.4 0.7 %pad_maximum_fusion.2 = bf16[2,2,3,16,128]{4,3,2,1,0:T(8,128)(2,1)S(1)} fusion(bf16[1,2,3,16,128]{4,3,2,1,0:T(8,128)(2,1)S(1)} %collective-permute-done, bf16[1,2,3,16,128]{4,3,2,1,0:T(8,128)(2,1)} %bitcast.15), kind=kLoop, calls=%fused_computation.2 | loop fusion | flops 24576 | bytes 98304 | tf_op jit(solution)/shard_map/concatenate | solution.py:351
  32.1 0.0 collective-permute-start.1
  32.1 4.1 %collective-permute-done.1 = bf16[2,2,3,16,128]{4,3,2,1,0:T(8,128)(2,1)S(1)} collective-permute-done((bf16[2,2,3,16,128]{4,3,2,1,0:T(8,128)(2,1)S(1)}, bf16[2,2,3,16,128]{4,3,2,1,0:T(8,128)(2,1)S(1)}, u32[]{:S(2)}, u32[]{:S(2)}) %collective-permute-start.1) | collective-permute-done | bytes 49184 | tf_op jit(solution)/shard_map/ppermute | solution.py:339
  36.2 0.8 %fusion = (bf16[1,4,2,3,16,128]{5,4,3,2,1,0:T(8,128)(2,1)S(1)}, bf16[4,2,3,16,128]{4,3,2,1,0:T(8,128)(2,1)S(1)}) fusion(bf16[2,2,3,16,128]{4,3,2,1,0:T(8,128)(2,1)S(1)} %collective-permute-done.1, bf16[1,2,3,16,128]{4,3,2,1,0:T(8,128)(2,1)S(1)} %collective-permute-done, bf16[1,2,3,16,128]{4,3,2,1,0:T(8,128)(2,1)} %bitcast.16), kind=kLoop, calls=%fused_computation.3 | loop fusion | flops 98304 | bytes 294912 | tf_op jit(solution)/shard_map/stack | solution.py:357
  37.0 1.6 %collective-permute-start.2 = (bf16[4,2,3,16,128]{4,3,2,1,0:T(8,128)(2,1)S(1)}, bf16[4,2,3,16,128]{4,3,2,1,0:T(8,128)(2,1)S(1)}, u32[]{:S(2)}, u32[]{:S(2)}) collective-permute-start(bf16[4,2,3,16,128]{4,3,2,1,0:T(8,128)(2,1)S(1)} %get-tuple-element.16), channel_id=1, source_target_pairs={{0,1},{1,0},{2,3},{3,2},{4,5},{5,4},{6,7},{7,6},{8,9},{9,8},{10,11... | collective-permute-start | bytes 294920 | tf_op jit(solution)/shard_map/ppermute | solution.py:342
  38.5 0.5 collective-permute-start.6
  39.1 2.0 %green_pieces.1 = bf16[6,3,128,128]{3,2,1,0:T(8,128)(2,1)} custom-call(s32[1]{0:T(128)} %bitcast.side_ref, bf16[6,6,128,256]{3,2,1,0:T(8,128)(2,1)} %bitcast.11), custom_call_target="tpu_custom_call" | custom-call | tf_op jit(solution)/shard_map/green_pieces/pallas_call | solution.py:146
  41.1 1.6 %collective-permute-start.7 = (bf16[6,3,128,128]{3,2,1,0:T(8,128)(2,1)}, bf16[6,3,128,128]{3,2,1,0:T(8,128)(2,1)S(1)}, u32[]{:S(2)}, u32[]{:S(2)}) collective-permute-start(bf16[6,3,128,128]{3,2,1,0:T(8,128)(2,1)} %green_pieces.1), channel_id=1, source_target_pairs={{0,1},{1,0},{2,3},{3,2},{4,5},{5,4},{6,7},{7,6},{8,9},{9,8},{10,11... | collective-permute-start | bytes 1769480 | tf_op jit(solution)/shard_map/ppermute | solution.py:342
  42.6 0.1 collective-permute-done.2
  42.7 1.5 %collective-permute-start.3 = (bf16[2,4,2,3,16,128]{5,4,3,2,1,0:T(8,128)(2,1)S(1)}, bf16[2,4,2,3,16,128]{5,4,3,2,1,0:T(8,128)(2,1)S(1)}, u32[]{:S(2)}, u32[]{:S(2)}) collective-permute-start(bf16[2,4,2,3,16,128]{5,4,3,2,1,0:T(8,128)(2,1)S(1)} %pad_maximum_fusion.near_ref), channel_id=1, source_target_pairs={{0,4},{2,6},{4,0},{6,2},{8,12},{10,14},{12,8},{14,10},{16,20},{18,... | collective-permute-start | bytes 589832 | tf_op jit(solution)/shard_map/ppermute | solution.py:339
  44.3 0.0 collective-permute-start.4
  44.3 4.2 %collective-permute-done.3.y_ref = bf16[2,4,2,3,16,128]{5,4,3,2,1,0:T(8,128)(2,1)S(1)} collective-permute-done((bf16[2,4,2,3,16,128]{5,4,3,2,1,0:T(8,128)(2,1)S(1)}, bf16[2,4,2,3,16,128]{5,4,3,2,1,0:T(8,128)(2,1)S(1)}, u32[]{:S(2)}, u32[]{:S(2)}) %collective-permute-start.3) | collective-permute-done | bytes 196640 | tf_op jit(solution)/shard_map/ppermute | solution.py:339
  48.5 1.4 %collective-permute-done.5.both_ref = bf16[2,4,2,3,16,128]{5,4,3,2,1,0:T(8,128)(2,1)S(1)} collective-permute-done((bf16[2,4,2,3,16,128]{5,4,3,2,1,0:T(8,128)(2,1)S(1)}, bf16[2,4,2,3,16,128]{5,4,3,2,1,0:T(8,128)(2,1)S(1)}, u32[]{:S(2)}, u32[]{:S(2)}) %collective-permute-start.5) | collective-permute-done | bytes 196640 | tf_op jit(solution)/shard_map/ppermute | solution.py:339
  49.9 5.5 %collective-permute-done.6.other_ref = bf16[6,3,128,128]{3,2,1,0:T(8,128)(2,1)} collective-permute-done((bf16[6,3,128,128]{3,2,1,0:T(8,128)(2,1)}, bf16[6,3,128,128]{3,2,1,0:T(8,128)(2,1)}, u32[]{:S(2)}, u32[]{:S(2)}) %collective-permute-start.6) | collective-permute-done | bytes 589856 | tf_op jit(solution)/shard_map/ppermute | solution.py:342
  55.5 1.7 %copy-done = bf16[2,3,128,6,256]{4,2,3,1,0:T(8,128)(2,1)S(1)} copy-done((bf16[2,3,128,6,256]{4,2,3,1,0:T(8,128)(2,1)S(1)}, bf16[2,3,128,6,256]{4,2,3,1,0:T(8,128)(2,1)}, u32[]{:S(2)}) %copy-start) | copy-done | bytes 2359320
  57.1 2.5 %held_first.1 = (f32[512,384]{1,0:T(8,128)S(1)}, f32[512,384]{1,0:T(8,128)S(1)}, bf16[2,512,768]{2,1,0:T(8,128)(2,1)S(1)}) custom-call(s32[1]{0:T(128)} %bitcast.2.me_ref, s32[1]{0:T(128)} %bitcast.side_ref, bf16[2,4,2,3,16,128]{5,4,3,2,1,0:T(8,128)(2,1)S(1)} %pad_maximum_fusion.near_ref, bf16[2,4,2,3,16,128]{5,4,3,2,1,0:T(8,128)(2,1)S(1)} %collective-permute-done.3.y_ref, ...), custom_call_target="tpu_custom_call" | custom-call | tf_op jit(solution)/shard_map/held_first/pallas_call | solution.py:255
  59.6 5.9 %collective-permute-done.7.other_ref = bf16[6,3,128,128]{3,2,1,0:T(8,128)(2,1)S(1)} collective-permute-done((bf16[6,3,128,128]{3,2,1,0:T(8,128)(2,1)}, bf16[6,3,128,128]{3,2,1,0:T(8,128)(2,1)S(1)}, u32[]{:S(2)}, u32[]{:S(2)}) %collective-permute-start.7) | collective-permute-done | bytes 589856 | tf_op jit(solution)/shard_map/ppermute | solution.py:342
  65.5 0.6 held_rest.1.rest_ref
  66.1 0.8 %combine.1 = f32[2,128]{1,0:T(2,128)} custom-call(bf16[16,12,16,128]{3,2,1,0:T(8,128)(2,1)S(1)} %all-to-all-done.strain_ref, f32[512,384]{1,0:T(8,128)S(1)} %get-tuple-element.12.first_ref, f32[512,384]{1,0:T(8,128)S(1)} %held_rest.1.rest_ref), custom_call_target="tpu_custom_call" | custom-call | tf_op jit(solution)/shard_map/combine/pallas_call | solution.py:316
  (5 shorter events, 0.0 us)
Async XLA Ops:
  2.0 64.1 %all-to-all-start = ((bf16[16,12,16,128]{3,2,1,0:T(8,128)(2,1)}), bf16[16,12,16,128]{3,2,1,0:T(8,128)(2,1)S(1)}, u32[]{:S(2)}, u32[]{:S(2)}) async-start(bf16[16,12,16,128]{3,2,1,0:T(8,128)(2,1)} %strain_pieces.1), calls=%async_computation | async-start | bytes 1572864 | tf_op jit(solution)/shard_map/all_to_all | solution.py:355
  12.1 19.3 %collective-permute-start = (bf16[1,2,3,16,128]{4,3,2,1,0:T(8,128)(2,1)}, bf16[1,2,3,16,128]{4,3,2,1,0:T(8,128)(2,1)S(1)}, u32[]{:S(2)}, u32[]{:S(2)}) collective-permute-start(bf16[1,2,3,16,128]{4,3,2,1,0:T(8,128)(2,1)} %bitcast.14), channel_id=1, source_target_pairs={{0,16},{2,18},{4,20},{6,22},{8,24},{10,26},{12,28},{14,30},{16,0},... | collective-permute-start | bytes 73736 | tf_op jit(solution)/shard_map/ppermute | solution.py:339
  32.1 4.1 %collective-permute-start.1 = (bf16[2,2,3,16,128]{4,3,2,1,0:T(8,128)(2,1)S(1)}, bf16[2,2,3,16,128]{4,3,2,1,0:T(8,128)(2,1)S(1)}, u32[]{:S(2)}, u32[]{:S(2)}) collective-permute-start(bf16[2,2,3,16,128]{4,3,2,1,0:T(8,128)(2,1)S(1)} %pad_maximum_fusion.2), channel_id=1, source_target_pairs={{0,8},{2,10},{4,12},{6,14},{8,0},{10,2},{12,4},{14,6},{16,24},{18,... | collective-permute-start | bytes 147464 | tf_op jit(solution)/shard_map/ppermute | solution.py:339
  37.0 5.7 %collective-permute-start.2 = (bf16[4,2,3,16,128]{4,3,2,1,0:T(8,128)(2,1)S(1)}, bf16[4,2,3,16,128]{4,3,2,1,0:T(8,128)(2,1)S(1)}, u32[]{:S(2)}, u32[]{:S(2)}) collective-permute-start(bf16[4,2,3,16,128]{4,3,2,1,0:T(8,128)(2,1)S(1)} %get-tuple-element.16), channel_id=1, source_target_pairs={{0,1},{1,0},{2,3},{3,2},{4,5},{5,4},{6,7},{7,6},{8,9},{9,8},{10,11... | collective-permute-start | bytes 294920 | tf_op jit(solution)/shard_map/ppermute | solution.py:342
  38.5 16.9 %collective-permute-start.6 = (bf16[6,3,128,128]{3,2,1,0:T(8,128)(2,1)}, bf16[6,3,128,128]{3,2,1,0:T(8,128)(2,1)}, u32[]{:S(2)}, u32[]{:S(2)}) collective-permute-start(bf16[6,3,128,128]{3,2,1,0:T(8,128)(2,1)} %get-tuple-element.11), channel_id=1, source_target_pairs={{0,1},{1,0},{2,3},{3,2},{4,5},{5,4},{6,7},{7,6},{8,9},{9,8},{10,11... | collective-permute-start | bytes 1769480 | tf_op jit(solution)/shard_map/ppermute | solution.py:342
  41.1 24.4 %collective-permute-start.7 = (bf16[6,3,128,128]{3,2,1,0:T(8,128)(2,1)}, bf16[6,3,128,128]{3,2,1,0:T(8,128)(2,1)S(1)}, u32[]{:S(2)}, u32[]{:S(2)}) collective-permute-start(bf16[6,3,128,128]{3,2,1,0:T(8,128)(2,1)} %green_pieces.1), channel_id=1, source_target_pairs={{0,1},{1,0},{2,3},{3,2},{4,5},{5,4},{6,7},{7,6},{8,9},{9,8},{10,11... | collective-permute-start | bytes 1769480 | tf_op jit(solution)/shard_map/ppermute | solution.py:342
  42.7 5.7 %collective-permute-start.3 = (bf16[2,4,2,3,16,128]{5,4,3,2,1,0:T(8,128)(2,1)S(1)}, bf16[2,4,2,3,16,128]{5,4,3,2,1,0:T(8,128)(2,1)S(1)}, u32[]{:S(2)}, u32[]{:S(2)}) collective-permute-start(bf16[2,4,2,3,16,128]{5,4,3,2,1,0:T(8,128)(2,1)S(1)} %pad_maximum_fusion.near_ref), channel_id=1, source_target_pairs={{0,4},{2,6},{4,0},{6,2},{8,12},{10,14},{12,8},{14,10},{16,20},{18,... | collective-permute-start | bytes 589832 | tf_op jit(solution)/shard_map/ppermute | solution.py:339
  44.3 4.2 %collective-permute-start.4 = (bf16[2,4,2,3,16,128]{5,4,3,2,1,0:T(8,128)(2,1)S(1)}, bf16[2,4,2,3,16,128]{5,4,3,2,1,0:T(8,128)(2,1)S(1)}, u32[]{:S(2)}, u32[]{:S(2)}) collective-permute-start(bf16[2,4,2,3,16,128]{5,4,3,2,1,0:T(8,128)(2,1)S(1)} %pad_maximum_fusion.near_ref), channel_id=1, source_target_pairs={{0,2},{2,0},{4,6},{6,4},{8,10},{10,8},{12,14},{14,12},{16,18},{18,... | collective-permute-start | bytes 589832 | tf_op jit(solution)/shard_map/ppermute | solution.py:339
  48.5 1.4 %collective-permute-start.5 = (bf16[2,4,2,3,16,128]{5,4,3,2,1,0:T(8,128)(2,1)S(1)}, bf16[2,4,2,3,16,128]{5,4,3,2,1,0:T(8,128)(2,1)S(1)}, u32[]{:S(2)}, u32[]{:S(2)}) collective-permute-start(bf16[2,4,2,3,16,128]{5,4,3,2,1,0:T(8,128)(2,1)S(1)} %collective-permute-done.3.y_ref), channel_id=1, source_target_pairs={{0,2},{2,0},{4,6},{6,4},{8,10},{10,8},{12,14},{14,12},{16,18},{18,... | collective-permute-start | bytes 589832 | tf_op jit(solution)/shard_map/ppermute | solution.py:339
  55.5 1.7 %copy-start = (bf16[2,3,128,6,256]{4,2,3,1,0:T(8,128)(2,1)S(1)}, bf16[2,3,128,6,256]{4,2,3,1,0:T(8,128)(2,1)}, u32[]{:S(2)}) copy-start(bf16[2,3,128,6,256]{4,2,3,1,0:T(8,128)(2,1)} %param.5) | copy-start | bytes 7077892

commit v2 on v0

--- a/solution.py
+++ b/solution.py
@@ -1,10 +1,17 @@
+import functools
+
 import jax
 import jax.numpy as jnp
 from jax import lax
+from jax.experimental import pallas as pl
+from jax.experimental.pallas import tpu as pltpu
 from jax.sharding import PartitionSpec as P
 
-
-def local(strain, green, weights, mask):
+LANES = 128
+COMPONENTS = 6
+
+
+def general(strain, green, weights, mask):
     masked = weights * mask.astype(jnp.bfloat16)[None, None]
     cells_dev = green.shape[4]
     station_count = green.shape[2]
@@ -41,6 +48,367 @@
     return lax.psum_scatter(partial_value, "st", scatter_dimension=1, tiled=True)
 
 
+VMEM_LIMIT = 24 * 1024 * 1024
+
+
+def params():
+    return pltpu.CompilerParams(vmem_limit_bytes=VMEM_LIMIT)
+
+
+def in_vmem():
+    return pl.BlockSpec(memory_space=pltpu.VMEM)
+
+
+def in_smem():
+    return pl.BlockSpec(memory_space=pltpu.SMEM)
+
+
+def stay(x):
+    return pltpu.with_memory_space_constraint(x, pltpu.HBM)
+
+
+def in_hbm():
+    return pl.BlockSpec(memory_space=pltpu.HBM)
+
+
+def green_moves(green_ref, buf, sent_ref, sems, out_sems, first, lane):
+    rows, size = sent_ref.shape[:2]
+    takes, gives = [], []
+    for i in range(rows):
+        takes.append(
+            pltpu.make_async_copy(
+                green_ref.at[i, pl.ds(first, size), :, pl.ds(lane, LANES)], buf.at[i], sems.at[i]
+            )
+        )
+        gives.append(pltpu.make_async_copy(buf.at[i], sent_ref.at[i], out_sems.at[i]))
+    return takes, gives
+
+
+def first_kernel(
+    st_count, side_ref, green_ref, weights_ref, mask_ref, strain_ref,
+    sent_ref, masked_ref, pieces_ref,
+    buf, weights_buf, mask_buf, pieces_buf, sems, out_sems, strain_sems, pieces_sems, small_sems,
+):
+    lane = pl.multiple_of((1 - side_ref[0]) * LANES, LANES)
+    small = [
+        pltpu.make_async_copy(weights_ref, weights_buf, small_sems.at[0]),
+        pltpu.make_async_copy(mask_ref, mask_buf, small_sems.at[1]),
+    ]
+    takes, gives = green_moves(green_ref, buf, sent_ref, sems, out_sems, 0, lane)
+    for i in range(pieces_ref.shape[0]):
+        lane = pl.multiple_of((i * st_count + side_ref[0]) * LANES, LANES)
+        takes.append(
+            pltpu.make_async_copy(
+                strain_ref.at[:, :, pl.ds(lane, LANES)], pieces_buf.at[i], strain_sems.at[i]
+            )
+        )
+        gives.append(pltpu.make_async_copy(pieces_buf.at[i], pieces_ref.at[i], pieces_sems.at[i]))
+    for copy in small + takes:
+        copy.start()
+    for copy in small:
+        copy.wait()
+    keep = mask_buf[...].astype(jnp.bfloat16)
+    for r in range(2):
+        for f in range(3):
+            masked_ref[r, f] = weights_buf[r, f] * keep
+    for take, give in zip(takes, gives):
+        take.wait()
+        give.start()
+    for copy in gives:
+        copy.wait()
+
+
+def first_pieces(side, green, weights, mask, strain, ev_count, st_count):
+    rows, _, stations, _ = green.shape
+    parts, events, _ = strain.shape
+    sent = (rows, COMPONENTS // 2, stations, LANES)
+    pieces = (ev_count, parts, events, LANES)
+    return pl.pallas_call(
+        functools.partial(first_kernel, st_count),
+        out_shape=(
+            jax.ShapeDtypeStruct(sent, green.dtype),
+            jax.ShapeDtypeStruct(weights.shape, weights.dtype),
+            jax.ShapeDtypeStruct(pieces, strain.dtype),
+        ),
+        in_specs=[in_smem(), in_hbm(), in_hbm(), in_hbm(), in_hbm()],
+        out_specs=(in_hbm(), in_vmem(), in_hbm()),
+        scratch_shapes=[
+            pltpu.VMEM(sent, green.dtype),
+            pltpu.VMEM(weights.shape, weights.dtype),
+            pltpu.VMEM(mask.shape, mask.dtype),
+            pltpu.VMEM(pieces, strain.dtype),
+            pltpu.SemaphoreType.DMA((rows,)),
+            pltpu.SemaphoreType.DMA((rows,)),
+            pltpu.SemaphoreType.DMA((ev_count,)),
+            pltpu.SemaphoreType.DMA((ev_count,)),
+            pltpu.SemaphoreType.DMA((2,)),
+        ],
+        compiler_params=params(),
+        name="first_pieces",
+    )(side, stay(green), stay(weights), stay(mask), stay(strain))
+
+
+def green_kernel(side_ref, green_ref, sent_ref, buf, sems, out_sems):
+    lane = pl.multiple_of((1 - side_ref[0]) * LANES, LANES)
+    takes, gives = green_moves(green_ref, buf, sent_ref, sems, out_sems, COMPONENTS // 2, lane)
+    for take in takes:
+        take.start()
+    for take, give in zip(takes, gives):
+        take.wait()
+        give.start()
+    for give in gives:
+        give.wait()
+
+
+def green_pieces(side, green):
+    rows, _, stations, _ = green.shape
+    shape = (rows, COMPONENTS // 2, stations, LANES)
+    return pl.pallas_call(
+        green_kernel,
+        out_shape=jax.ShapeDtypeStruct(shape, green.dtype),
+        in_specs=[in_smem(), in_hbm()],
+        out_specs=in_hbm(),
+        scratch_shapes=[
+            pltpu.VMEM(shape, green.dtype),
+            pltpu.SemaphoreType.DMA((rows,)),
+            pltpu.SemaphoreType.DMA((rows,)),
+        ],
+        compiler_params=params(),
+        name="green_pieces",
+    )(side, stay(green))
+
+
+def own_kernel(side_ref, green_ref, own_ref, sems):
+    lane = pl.multiple_of(side_ref[0] * LANES, LANES)
+    copies = [
+        pltpu.make_async_copy(green_ref.at[i, :, :, pl.ds(lane, LANES)], own_ref.at[i], sems.at[i])
+        for i in range(own_ref.shape[0])
+    ]
+    for copy in copies:
+        copy.start()
+    for copy in copies:
+        copy.wait()
+
+
+def own_green(side, green):
+    rows, parts, stations, _ = green.shape
+    return pl.pallas_call(
+        own_kernel,
+        out_shape=jax.ShapeDtypeStruct((rows, parts, stations, LANES), green.dtype),
+        in_specs=[in_smem(), in_hbm()],
+        out_specs=in_vmem(),
+        scratch_shapes=[pltpu.SemaphoreType.DMA((rows,))],
+        compiler_params=params(),
+        name="own_green",
+    )(side, stay(green))
+
+
+def stacked(block_ref, components):
+    columns = [
+        jnp.concatenate([block_ref[i, c] for i in range(block_ref.shape[0])], axis=0)
+        for c in components
+    ]
+    return columns[0] if len(columns) == 1 else jnp.concatenate(columns, axis=1)
+
+
+def turned(block_ref, c):
+    kinds = block_ref.shape[0] // 2
+    real = jnp.concatenate([block_ref[i, c] for i in range(kinds)], axis=0)
+    imag = jnp.concatenate([block_ref[kinds + i, c] for i in range(kinds)], axis=0)
+    upper = jnp.concatenate([real, imag], axis=1)
+    lower = jnp.concatenate([-imag, real], axis=1)
+    return jnp.concatenate([upper, lower], axis=0)
+
+
+def product(left, right):
+    return jnp.dot(left, right, preferred_element_type=jnp.float32)
+
+
+def held_half(w_refs, own_ref, other_ref, held_ref, before_ref, rows_ref, lhs):
+    _, far, _, _, events, stations = w_refs[0].shape
+    half = 2 * far * events
+    for k, w_ref in enumerate(w_refs):
+        for z in range(far):
+            start = (k * far + z) * events
+            rows = slice(start, start + events)
+            low = slice(half + start, half + start + events)
+            for f in range(3):
+                first = slice(f * stations, (f + 1) * stations)
+                second = slice((3 + f) * stations, (4 + f) * stations)
+                for h in range(2):
+                    real = w_ref[h, z, 0, f]
+                    imag = w_ref[h, z, 1, f]
+                    lhs[h, rows, first] = real
+                    lhs[h, low, first] = imag
+                    lhs[h, rows, second] = -imag
+                    lhs[h, low, second] = real
+                rows_ref[rows, first] = real
+                rows_ref[rows, second] = imag
+    wide = 2 * LANES
+    held_ref[:, :wide] = product(lhs[0], stacked(own_ref, (0, 1))) + product(
+        lhs[1], stacked(other_ref, (0, 1))
+    )
+    middle = product(lhs[0], stacked(own_ref, (2, 3)))
+    held_ref[:, wide:] = middle[:, :LANES] + product(lhs[1], stacked(other_ref, (2,)))
+    before_ref[:, :LANES] = middle[:, LANES:]
+    before_ref[:, LANES:] = product(lhs[0], stacked(own_ref, (4, 5)))
+
+
+def held_kernel(near_ref, core_ref, own_ref, other_ref, held_ref, before_ref, rows_ref, lhs):
+    held_half((near_ref, core_ref), own_ref, other_ref, held_ref, before_ref, rows_ref, lhs)
+
+
+def held(near, core, own, other):
+    _, far, _, _, events, stations = near.shape
+    rows = 4 * far * events
+    part = jax.ShapeDtypeStruct((rows, 3 * LANES), jnp.float32)
+    return pl.pallas_call(
+        held_kernel,
+        out_shape=(part, part, jax.ShapeDtypeStruct((rows // 2, 6 * stations), jnp.bfloat16)),
+        in_specs=[in_vmem()] * 4,
+        out_specs=(in_vmem(),) * 3,
+        scratch_shapes=[pltpu.VMEM((2, rows, 6 * stations), jnp.bfloat16)],
+        compiler_params=params(),
+    )(near, core, own, other)
+
+
+def rest_kernel(
+    rows_a_ref, rows_b_ref, held_a_ref, held_b_ref, before_a_ref, before_b_ref, other_ref,
+    full_ref, left,
+):
+    half = rows_a_ref.shape[0]
+    base = held_a_ref.shape[1]
+    full_ref[0, :, :base] = held_a_ref[...]
+    full_ref[1, :, :base] = held_b_ref[...]
+    left[:half] = rows_a_ref[...]
+    left[half:] = rows_b_ref[...]
+    for c in range(COMPONENTS // 2):
+        lanes = slice(c * LANES, (c + 1) * LANES)
+        fresh = product(left[...], turned(other_ref, c))
+        for y, before_ref in enumerate((before_a_ref, before_b_ref)):
+            mine = slice(y * half, (y + 1) * half)
+            out = slice(base + c * LANES, base + (c + 1) * LANES)
+            full_ref[y, :half, out] = before_ref[:half, lanes] + fresh[mine, :LANES]
+            full_ref[y, half:, out] = before_ref[half:, lanes] + fresh[mine, LANES:]
+
+
+def held_rest(rows_a, rows_b, held_a, held_b, before_a, before_b, other):
+    half, depth = rows_a.shape
+    return pl.pallas_call(
+        rest_kernel,
+        out_shape=jax.ShapeDtypeStruct((2, 2 * half, COMPONENTS * LANES), jnp.float32),
+        in_specs=[in_vmem()] * 7,
+        out_specs=in_vmem(),
+        scratch_shapes=[pltpu.VMEM((2 * half, depth), rows_a.dtype)],
+        compiler_params=params(),
+        name="held_rest",
+    )(rows_a, rows_b, held_a, held_b, before_a, before_b, other)
+
+
+def combine_kernel(bits, me_ref, strain_ref, full_ref, o_ref):
+    count, _, events, _ = strain_ref.shape
+    far = count // 4
+    half = count // 2 * events
+    trace = jnp.zeros((events, LANES), jnp.float32)
+    normal = jnp.zeros((events, LANES), jnp.float32)
+    cross = jnp.zeros((events, LANES), jnp.float32)
+    for y in range(2):
+        for k in range(2):
+            for z in range(far):
+                offset = y * 2 + k + sum(bit for place, bit in enumerate(bits) if z >> place & 1)
+                block = me_ref[0] ^ offset
+                start = (k * far + z) * events
+                rows = slice(start, start + events)
+                low = slice(half + start, half + start + events)
+                sums = None
+                for c in range(COMPONENTS):
+                    real = strain_ref[block, c].astype(jnp.float32)
+                    imag = strain_ref[block, COMPONENTS + c].astype(jnp.float32)
+                    lanes = slice(c * LANES, (c + 1) * LANES)
+                    held_real = full_ref[y, rows, lanes]
+                    held_imag = full_ref[y, low, lanes]
+                    term = real * held_real - imag * held_imag
+                    if c < 3:
+                        normal = normal + term
+                        four = (real, imag, held_real, held_imag)
+                        sums = four if sums is None else tuple(u + v for u, v in zip(sums, four))
+                    else:
+                        cross = cross + term
+                trace = trace + (sums[0] * sums[2] - sums[1] * sums[3])
+    o_ref[0:1, :] = jnp.sum(trace, axis=0, keepdims=True)
+    o_ref[1:2, :] = jnp.sum(normal + 2.0 * cross, axis=0, keepdims=True)
+
+
+def combine(bits, me, strain, full):
+    return pl.pallas_call(
+        functools.partial(combine_kernel, bits),
+        out_shape=jax.ShapeDtypeStruct((2, LANES), jnp.float32),
+        in_specs=[in_smem()] + [in_vmem()] * 2,
+        out_specs=in_vmem(),
+        compiler_params=params(),
+        name="combine",
+    )(me, strain, full)
+
+
+def paired(strain, green, weights, mask):
+    return paired_steps(strain, green, weights, mask)
+
+
+def paired_steps(strain, green, weights, mask):
+    ev_count = lax.axis_size("ev")
+    st_count = lax.axis_size("st")
+    event_rows = strain.shape[2]
+    station_count = green.shape[2]
+    me = lax.axis_index("ev").astype(jnp.int32)[None]
+    side = lax.axis_index("st").astype(jnp.int32)[None]
+
+    def hop(x, bit):
+        return lax.ppermute(x, "ev", [(i, i ^ bit) for i in range(ev_count)])
+
+    def swap(x):
+        return lax.ppermute(x, "st", [(0, 1), (1, 0)])
+
+    green = jnp.transpose(green, (0, 1, 3, 2, 4)).reshape(6, COMPONENTS, station_count, 2 * LANES)
+    sent_first, masked, pieces = first_pieces(
+        side, green, weights, mask, strain.reshape(12, event_rows, -1), ev_count, st_count
+    )
+    other_first = swap(sent_first)
+    gathered, bits = masked[None], []
+    bit = ev_count // 2
+    while bit > 2:
+        gathered = jnp.concatenate([gathered, hop(gathered, bit)])
+        bits.append(bit)
+        bit //= 2
+    moved = lax.all_to_all(pieces, "ev", 0, 0, tiled=True)
+
+    near = jnp.stack([gathered, swap(gathered)])
+    sent_rest = green_pieces(side, green)
+    other_rest = swap(sent_rest)
+    y = hop(near, 2)
+    core = hop(near, 1)
+    both = hop(y, 1)
+
+    own = own_green(side, green)
+    held_a, before_a, rows_a = held(near, core, own, other_first)
+    held_b, before_b, rows_b = held(y, both, own, other_first)
+    full = held_rest(rows_a, rows_b, held_a, held_b, before_a, before_b, other_rest)
+    return combine(bits, me, moved, full)
+
+
+def local(strain, green, weights, mask):
+    ev_count = lax.axis_size("ev")
+    st_count = lax.axis_size("st")
+    fits = (
+        st_count == 2
+        and ev_count >= 8
+        and ev_count & (ev_count - 1) == 0
+        and green.shape[4] == st_count * LANES
+        and green.shape[2] % LANES == 0
+        and strain.shape[2] % 16 == 0
+    )
+    return (paired if fits else general)(strain, green, weights, mask)
+
+
 def solution(mesh):
     placed = (
         P(None, None, "ev", None),

time: 144 us -> 66.5 us (0.46)
  local copies, waits for them, and re-layouts: 68.5 us -> 0 us
  blocking collectives: 22.4 us -> 0 us
  waiting for transfers between devices: 23.4 us -> 39.4 us
  between operations: 13.6 us -> 0.11 us
  Pallas kernels: 0 us -> 10.6 us
  starting transfers between devices: 7.63 us -> 15.9 us
  other arithmetic: 5.83 us -> 0.04 us
  matrix products: 1.83 us -> 0 us
    ppermute x0 -> x8, waiting for transfers between devices: none -> 39.4 us  [the longest x5 27.4 us: hop(): return lax.ppermute(x, 'ev', [(i, i ^ bit) for i in range(ev_count)])]
    unnamed x13 -> x0, local copies, waits for them, and re-layouts: 30.6 us -> none
    all_gather x1 -> x0, blocking collectives: 22.4 us -> none  [local(): weight_rows = lax.all_gather(masked, 'ev', axis=2, tiled=True)]
    all_to_all x1, waiting for transfers between devices: 15.5 us -> 0.01 us  [paired_steps(): moved = lax.all_to_all(pieces, 'ev', 0, 0, tiled=True)]
    all_to_all x1 -> x0, local copies, waits for them, and re-layouts: 14.8 us -> none  [local(): lax.all_to_all(selected, 'ev', split_axis=3, concat_axis=2, tiled=True)]
    reshape x2 -> x0, local copies, waits for them, and re-layouts: 14.4 us -> none  [the longest x1 11.5 us: local(): selected = selected.reshape(2, 6, event_rows, ev_count * sub_cells)]
    pallas_call x0 -> x7, Pallas kernels: none -> 10.6 us  [the longest x2 3.26 us: held(): pl.pallas_call(held_kernel, out_shape=(part, part, jax.ShapeDtypeStruct((...]
    ppermute x0 -> x8, starting transfers between devices: none -> 8.52 us  [the longest x5 4.87 us: hop(): return lax.ppermute(x, 'ev', [(i, i ^ bit) for i in range(ev_count)])]
  transfers between devices with their start and end apart: 3 -> 9, of which waited for: 2 -> 6; matrix products, arithmetic and copies ran while one was open for 10% -> 0% of each run, Pallas kernels for 0% -> 11%
where the time goes in v2:
time: 66.5 us; the launch traced here: 66.1 us
  waiting for transfers between devices  39.4 us (59%)
  starting transfers between devices  15.9 us (24%)
  Pallas kernels  10.6 us (16%)
    ppermute x5, waiting for transfers between devices, hop(): return lax.ppermute(x, 'ev', [(i, i ^ bit) for i in range(ev_count)])  27.4 us
    ppermute x3, waiting for transfers between devices, swap(): return lax.ppermute(x, 'st', [(0, 1), (1, 0)])  12 us
    all_to_all x1, starting transfers between devices, paired_steps(): moved = lax.all_to_all(pieces, 'ev', 0, 0, tiled=True)  7.43 us
    ppermute x5, starting transfers between devices, hop(): return lax.ppermute(x, 'ev', [(i, i ^ bit) for i in range(ev_count)])  4.87 us
    ppermute x3, starting transfers between devices, swap(): return lax.ppermute(x, 'st', [(0, 1), (1, 0)])  3.65 us
    pallas_call x2, Pallas kernels, held(): pl.pallas_call(held_kernel, out_shape=(part, part, jax.ShapeDtypeStruct((...  3.26 us
    pallas_call x1, Pallas kernels, first_pieces(): pl.pallas_call(functools.partial(first_kernel, st_count), out_shape=(jax....  2.76 us
    pallas_call x1, Pallas kernels, green_pieces(): pl.pallas_call(green_kernel, out_shape=jax.ShapeDtypeStruct(shape, green....  1.87 us
  transfers between devices with their start and end apart: 9, of which 6 were waited for; matrix products, arithmetic and copies ran while one was open for 0% of the time, Pallas kernels for 11%

profile of v2, /device:TPU:0, one launch (start us, length us, event | category | flops | bytes accessed | tf_op | source)
XLA Modules:
  0.0 66.1 jit_solution(17943694961860774016)
XLA Ops:
  0.0 2.8 %first_pieces.1 = (bf16[6,3,128,128]{3,2,1,0:T(8,128)(2,1)}, bf16[2,3,16,128]{3,2,1,0:T(8,128)(2,1)S(1)}, bf16[16,12,16,128]{3,2,1,0:T(8,128)(2,1)}) custom-call(s32[1]{0:T(128)} %bitcast.1.side_ref, bf16[6,6,128,256]{3,2,1,0:T(8,128)(2,1)} %bitcast.13, bf16[2,3,16,128]{3,2,1,0:T(8,128)(2,1)} %weights_ref.1, s32[16,128]{1,0:T(8,128)} %mask_ref.1, ...), custom_call_target="tpu_custom_call" | custom-call | tf_op jit(solution)/shard_map/first_pieces/pallas_call | solution.py:126
  2.8 7.4 %all-to-all-start = ((bf16[16,12,16,128]{3,2,1,0:T(8,128)(2,1)}), bf16[16,12,16,128]{3,2,1,0:T(8,128)(2,1)S(1)}, u32[]{:S(2)}, u32[]{:S(2)}) async-start(bf16[16,12,16,128]{3,2,1,0:T(8,128)(2,1)} %get-tuple-element.14), calls=%async_computation | async-start | bytes 1572864 | tf_op jit(solution)/shard_map/all_to_all | solution.py:382
  10.2 2.8 %collective-permute-start = (bf16[1,2,3,16,128]{4,3,2,1,0:T(8,128)(2,1)S(1)}, bf16[1,2,3,16,128]{4,3,2,1,0:T(8,128)(2,1)S(1)}, u32[]{:S(2)}, u32[]{:S(2)}) collective-permute-start(bf16[1,2,3,16,128]{4,3,2,1,0:T(8,128)(2,1)S(1)} %bitcast.10), channel_id=1, source_target_pairs={{0,16},{2,18},{4,20},{6,22},{8,24},{10,26},{12,28},{14,30},{16,0},... | collective-permute-start | bytes 73736 | tf_op jit(solution)/shard_map/ppermute | solution.py:366
  13.0 19.1 %collective-permute-done = bf16[1,2,3,16,128]{4,3,2,1,0:T(8,128)(2,1)S(1)} collective-permute-done((bf16[1,2,3,16,128]{4,3,2,1,0:T(8,128)(2,1)S(1)}, bf16[1,2,3,16,128]{4,3,2,1,0:T(8,128)(2,1)S(1)}, u32[]{:S(2)}, u32[]{:S(2)}) %collective-permute-start) | collective-permute-done | bytes 24608 | tf_op jit(solution)/shard_map/ppermute | solution.py:366
  32.2 0.0 collective-permute-start.1
  32.2 4.1 %collective-permute-done.1 = bf16[2,2,3,16,128]{4,3,2,1,0:T(8,128)(2,1)S(1)} collective-permute-done((bf16[2,2,3,16,128]{4,3,2,1,0:T(8,128)(2,1)S(1)}, bf16[2,2,3,16,128]{4,3,2,1,0:T(8,128)(2,1)S(1)}, u32[]{:S(2)}, u32[]{:S(2)}) %collective-permute-start.1) | collective-permute-done | bytes 49184 | tf_op jit(solution)/shard_map/ppermute | solution.py:366
  36.3 1.6 %collective-permute-start.2 = (bf16[4,2,3,16,128]{4,3,2,1,0:T(8,128)(2,1)S(1)}, bf16[4,2,3,16,128]{4,3,2,1,0:T(8,128)(2,1)S(1)}, u32[]{:S(2)}, u32[]{:S(2)}) collective-permute-start(bf16[4,2,3,16,128]{4,3,2,1,0:T(8,128)(2,1)S(1)} %get-tuple-element.24), channel_id=1, source_target_pairs={{0,1},{1,0},{2,3},{3,2},{4,5},{5,4},{6,7},{7,6},{8,9},{9,8},{10,11... | collective-permute-start | bytes 294920 | tf_op jit(solution)/shard_map/ppermute | solution.py:369
  37.8 0.5 collective-permute-start.4
  38.4 1.9 %green_pieces.1 = bf16[6,3,128,128]{3,2,1,0:T(8,128)(2,1)} custom-call(s32[1]{0:T(128)} %bitcast.1.side_ref, bf16[6,6,128,256]{3,2,1,0:T(8,128)(2,1)} %bitcast.14), custom_call_target="tpu_custom_call" | custom-call | tf_op jit(solution)/shard_map/green_pieces/pallas_call | solution.py:166
  40.2 1.6 %collective-permute-start.7 = (bf16[6,3,128,128]{3,2,1,0:T(8,128)(2,1)}, bf16[6,3,128,128]{3,2,1,0:T(8,128)(2,1)S(1)}, u32[]{:S(2)}, u32[]{:S(2)}) collective-permute-start(bf16[6,3,128,128]{3,2,1,0:T(8,128)(2,1)} %green_pieces.1), channel_id=1, source_target_pairs={{0,1},{1,0},{2,3},{3,2},{4,5},{5,4},{6,7},{7,6},{8,9},{9,8},{10,11... | collective-permute-start | bytes 1769480 | tf_op jit(solution)/shard_map/ppermute | solution.py:369
  41.8 0.2 collective-permute-done.2
  42.0 1.5 %collective-permute-start.5 = (bf16[2,4,2,3,16,128]{5,4,3,2,1,0:T(8,128)(2,1)S(1)}, bf16[2,4,2,3,16,128]{5,4,3,2,1,0:T(8,128)(2,1)S(1)}, u32[]{:S(2)}, u32[]{:S(2)}) collective-permute-start(bf16[2,4,2,3,16,128]{5,4,3,2,1,0:T(8,128)(2,1)S(1)} %pad_maximum_fusion.near_ref), channel_id=1, source_target_pairs={{0,4},{2,6},{4,0},{6,2},{8,12},{10,14},{12,8},{14,10},{16,20},{18,... | collective-permute-start | bytes 589832 | tf_op jit(solution)/shard_map/ppermute | solution.py:366
  43.6 4.2 %collective-permute-done.5.near_ref = bf16[2,4,2,3,16,128]{5,4,3,2,1,0:T(8,128)(2,1)S(1)} collective-permute-done((bf16[2,4,2,3,16,128]{5,4,3,2,1,0:T(8,128)(2,1)S(1)}, bf16[2,4,2,3,16,128]{5,4,3,2,1,0:T(8,128)(2,1)S(1)}, u32[]{:S(2)}, u32[]{:S(2)}) %collective-permute-start.5) | collective-permute-done | bytes 196640 | tf_op jit(solution)/shard_map/ppermute | solution.py:366
  47.8 0.0 collective-permute-start.6
  47.8 0.5 collective-permute-start.3
  48.3 1.4 %own_green.1.own_ref = bf16[6,6,128,128]{3,2,1,0:T(8,128)(2,1)S(1)} custom-call(s32[1]{0:T(128)} %bitcast.1.side_ref, bf16[6,6,128,256]{3,2,1,0:T(8,128)(2,1)} %bitcast.15), custom_call_target="tpu_custom_call" | custom-call | tf_op jit(solution)/shard_map/own_green/pallas_call | solution.py:195
  49.7 0.0 collective-permute-done.6.core_ref
  49.7 5.0 %collective-permute-done.4.other_ref = bf16[6,3,128,128]{3,2,1,0:T(8,128)(2,1)S(1)} collective-permute-done((bf16[6,3,128,128]{3,2,1,0:T(8,128)(2,1)}, bf16[6,3,128,128]{3,2,1,0:T(8,128)(2,1)S(1)}, u32[]{:S(2)}, u32[]{:S(2)}) %collective-permute-start.4) | collective-permute-done | bytes 589856 | tf_op jit(solution)/shard_map/ppermute | solution.py:369
  54.6 1.6 %shard_map.47 = (f32[256,384]{1,0:T(8,128)S(1)}, f32[256,384]{1,0:T(8,128)S(1)}, bf16[128,768]{1,0:T(8,128)(2,1)S(1)}) custom-call(bf16[2,4,2,3,16,128]{5,4,3,2,1,0:T(8,128)(2,1)S(1)} %collective-permute-done.5.near_ref, bf16[2,4,2,3,16,128]{5,4,3,2,1,0:T(8,128)(2,1)} %collective-permute-done.6.core_ref, bf16[6,6,128,128]{3,2,1,0:T(8,128)(2,1)S(1)} %own_green.1.own_ref, ...), custom_call_target="tpu_custom_call" | custom-call | tf_op jit(solution)/shard_map/pallas_call | solution.py:265
  56.3 0.0 collective-permute-done.3.core_ref
  56.3 1.6 %shard_map.46 = (f32[256,384]{1,0:T(8,128)S(1)}, f32[256,384]{1,0:T(8,128)S(1)}, bf16[128,768]{1,0:T(8,128)(2,1)S(1)}) custom-call(bf16[2,4,2,3,16,128]{5,4,3,2,1,0:T(8,128)(2,1)S(1)} %pad_maximum_fusion.near_ref, bf16[2,4,2,3,16,128]{5,4,3,2,1,0:T(8,128)(2,1)} %collective-permute-done.3.core_ref, bf16[6,6,128,128]{3,2,1,0:T(8,128)(2,1)S(1)} %own_green.1.own_ref, ...), custom_call_target="tpu_custom_call" | custom-call | tf_op jit(solution)/shard_map/pallas_call | solution.py:265
  57.9 6.9 %collective-permute-done.7.other_ref = bf16[6,3,128,128]{3,2,1,0:T(8,128)(2,1)S(1)} collective-permute-done((bf16[6,3,128,128]{3,2,1,0:T(8,128)(2,1)}, bf16[6,3,128,128]{3,2,1,0:T(8,128)(2,1)S(1)}, u32[]{:S(2)}, u32[]{:S(2)}) %collective-permute-start.7) | collective-permute-done | bytes 589856 | tf_op jit(solution)/shard_map/ppermute | solution.py:369
  64.8 0.6 held_rest.1.full_ref
  65.4 0.8 %combine.1 = f32[2,128]{1,0:T(2,128)} custom-call(s32[1]{0:T(128)} %bitcast.me_ref, bf16[16,12,16,128]{3,2,1,0:T(8,128)(2,1)S(1)} %all-to-all-done.strain_ref, f32[2,256,768]{2,1,0:T(8,128)S(1)} %held_rest.1.full_ref), custom_call_target="tpu_custom_call" | custom-call | tf_op jit(solution)/shard_map/combine/pallas_call | solution.py:343
  (4 shorter events, 0.0 us)
Async XLA Ops:
  2.8 62.6 %all-to-all-start = ((bf16[16,12,16,128]{3,2,1,0:T(8,128)(2,1)}), bf16[16,12,16,128]{3,2,1,0:T(8,128)(2,1)S(1)}, u32[]{:S(2)}, u32[]{:S(2)}) async-start(bf16[16,12,16,128]{3,2,1,0:T(8,128)(2,1)} %get-tuple-element.14), calls=%async_computation | async-start | bytes 1572864 | tf_op jit(solution)/shard_map/all_to_all | solution.py:382
  10.2 21.9 %collective-permute-start = (bf16[1,2,3,16,128]{4,3,2,1,0:T(8,128)(2,1)S(1)}, bf16[1,2,3,16,128]{4,3,2,1,0:T(8,128)(2,1)S(1)}, u32[]{:S(2)}, u32[]{:S(2)}) collective-permute-start(bf16[1,2,3,16,128]{4,3,2,1,0:T(8,128)(2,1)S(1)} %bitcast.10), channel_id=1, source_target_pairs={{0,16},{2,18},{4,20},{6,22},{8,24},{10,26},{12,28},{14,30},{16,0},... | collective-permute-start | bytes 73736 | tf_op jit(solution)/shard_map/ppermute | solution.py:366
  32.2 4.1 %collective-permute-start.1 = (bf16[2,2,3,16,128]{4,3,2,1,0:T(8,128)(2,1)S(1)}, bf16[2,2,3,16,128]{4,3,2,1,0:T(8,128)(2,1)S(1)}, u32[]{:S(2)}, u32[]{:S(2)}) collective-permute-start(bf16[2,2,3,16,128]{4,3,2,1,0:T(8,128)(2,1)S(1)} %pad_maximum_fusion.2), channel_id=1, source_target_pairs={{0,8},{2,10},{4,12},{6,14},{8,0},{10,2},{12,4},{14,6},{16,24},{18,... | collective-permute-start | bytes 147464 | tf_op jit(solution)/shard_map/ppermute | solution.py:366
  36.3 5.7 %collective-permute-start.2 = (bf16[4,2,3,16,128]{4,3,2,1,0:T(8,128)(2,1)S(1)}, bf16[4,2,3,16,128]{4,3,2,1,0:T(8,128)(2,1)S(1)}, u32[]{:S(2)}, u32[]{:S(2)}) collective-permute-start(bf16[4,2,3,16,128]{4,3,2,1,0:T(8,128)(2,1)S(1)} %get-tuple-element.24), channel_id=1, source_target_pairs={{0,1},{1,0},{2,3},{3,2},{4,5},{5,4},{6,7},{7,6},{8,9},{9,8},{10,11... | collective-permute-start | bytes 294920 | tf_op jit(solution)/shard_map/ppermute | solution.py:369
  37.8 16.8 %collective-permute-start.4 = (bf16[6,3,128,128]{3,2,1,0:T(8,128)(2,1)}, bf16[6,3,128,128]{3,2,1,0:T(8,128)(2,1)S(1)}, u32[]{:S(2)}, u32[]{:S(2)}) collective-permute-start(bf16[6,3,128,128]{3,2,1,0:T(8,128)(2,1)} %get-tuple-element.16), channel_id=1, source_target_pairs={{0,1},{1,0},{2,3},{3,2},{4,5},{5,4},{6,7},{7,6},{8,9},{9,8},{10,11... | collective-permute-start | bytes 1769480 | tf_op jit(solution)/shard_map/ppermute | solution.py:369
  40.2 24.5 %collective-permute-start.7 = (bf16[6,3,128,128]{3,2,1,0:T(8,128)(2,1)}, bf16[6,3,128,128]{3,2,1,0:T(8,128)(2,1)S(1)}, u32[]{:S(2)}, u32[]{:S(2)}) collective-permute-start(bf16[6,3,128,128]{3,2,1,0:T(8,128)(2,1)} %green_pieces.1), channel_id=1, source_target_pairs={{0,1},{1,0},{2,3},{3,2},{4,5},{5,4},{6,7},{7,6},{8,9},{9,8},{10,11... | collective-permute-start | bytes 1769480 | tf_op jit(solution)/shard_map/ppermute | solution.py:369
  42.0 5.7 %collective-permute-start.5 = (bf16[2,4,2,3,16,128]{5,4,3,2,1,0:T(8,128)(2,1)S(1)}, bf16[2,4,2,3,16,128]{5,4,3,2,1,0:T(8,128)(2,1)S(1)}, u32[]{:S(2)}, u32[]{:S(2)}) collective-permute-start(bf16[2,4,2,3,16,128]{5,4,3,2,1,0:T(8,128)(2,1)S(1)} %pad_maximum_fusion.near_ref), channel_id=1, source_target_pairs={{0,4},{2,6},{4,0},{6,2},{8,12},{10,14},{12,8},{14,10},{16,20},{18,... | collective-permute-start | bytes 589832 | tf_op jit(solution)/shard_map/ppermute | solution.py:366
  47.8 1.9 %collective-permute-start.6 = (bf16[2,4,2,3,16,128]{5,4,3,2,1,0:T(8,128)(2,1)S(1)}, bf16[2,4,2,3,16,128]{5,4,3,2,1,0:T(8,128)(2,1)}, u32[]{:S(2)}, u32[]{:S(2)}) collective-permute-start(bf16[2,4,2,3,16,128]{5,4,3,2,1,0:T(8,128)(2,1)S(1)} %collective-permute-done.5.near_ref), channel_id=1, source_target_pairs={{0,2},{2,0},{4,6},{6,4},{8,10},{10,8},{12,14},{14,12},{16,18},{18,... | collective-permute-start | bytes 589832 | tf_op jit(solution)/shard_map/ppermute | solution.py:366
  47.8 8.5 %collective-permute-start.3 = (bf16[2,4,2,3,16,128]{5,4,3,2,1,0:T(8,128)(2,1)S(1)}, bf16[2,4,2,3,16,128]{5,4,3,2,1,0:T(8,128)(2,1)}, u32[]{:S(2)}, u32[]{:S(2)}) collective-permute-start(bf16[2,4,2,3,16,128]{5,4,3,2,1,0:T(8,128)(2,1)S(1)} %pad_maximum_fusion.near_ref), channel_id=1, source_target_pairs={{0,2},{2,0},{4,6},{6,4},{8,10},{10,8},{12,14},{14,12},{16,18},{18,... | collective-permute-start | bytes 589832 | tf_op jit(solution)/shard_map/ppermute | solution.py:366

commit v3 on v2

--- a/solution.py
+++ b/solution.py
@@ -305,7 +305,7 @@
     )(rows_a, rows_b, held_a, held_b, before_a, before_b, other)
 
 
-def combine_kernel(bits, me_ref, strain_ref, full_ref, o_ref):
+def combine_kernel(me_ref, strain_ref, full_ref, o_ref):
     count, _, events, _ = strain_ref.shape
     far = count // 4
     half = count // 2 * events
@@ -315,7 +315,7 @@
     for y in range(2):
         for k in range(2):
             for z in range(far):
-                offset = y * 2 + k + sum(bit for place, bit in enumerate(bits) if z >> place & 1)
+                offset = 4 * z + 2 * y + k
                 block = me_ref[0] ^ offset
                 start = (k * far + z) * events
                 rows = slice(start, start + events)
@@ -339,9 +339,9 @@
     o_ref[1:2, :] = jnp.sum(normal + 2.0 * cross, axis=0, keepdims=True)
 
 
-def combine(bits, me, strain, full):
-    return pl.pallas_call(
-        functools.partial(combine_kernel, bits),
+def combine(me, strain, full):
+    return pl.pallas_call(
+        combine_kernel,
         out_shape=jax.ShapeDtypeStruct((2, LANES), jnp.float32),
         in_specs=[in_smem()] + [in_vmem()] * 2,
         out_specs=in_vmem(),
@@ -373,12 +373,7 @@
         side, green, weights, mask, strain.reshape(12, event_rows, -1), ev_count, st_count
     )
     other_first = swap(sent_first)
-    gathered, bits = masked[None], []
-    bit = ev_count // 2
-    while bit > 2:
-        gathered = jnp.concatenate([gathered, hop(gathered, bit)])
-        bits.append(bit)
-        bit //= 2
+    gathered = jnp.stack([masked] + [hop(masked, bit) for bit in range(4, ev_count, 4)])
     moved = lax.all_to_all(pieces, "ev", 0, 0, tiled=True)
 
     near = jnp.stack([gathered, swap(gathered)])
@@ -392,7 +387,7 @@
     held_a, before_a, rows_a = held(near, core, own, other_first)
     held_b, before_b, rows_b = held(y, both, own, other_first)
     full = held_rest(rows_a, rows_b, held_a, held_b, before_a, before_b, other_rest)
-    return combine(bits, me, moved, full)
+    return combine(me, moved, full)
 
 
 def local(strain, green, weights, mask):

time: 66.5 us -> 64.1 us (0.964)
  waiting for transfers between devices: 39.4 us -> 35.4 us
  starting transfers between devices: 15.9 us -> 17.6 us
    ppermute x5 -> x6, waiting for transfers between devices: 27.4 us -> 22.5 us  [hop(): return lax.ppermute(x, 'ev', [(i, i ^ bit) for i in range(ev_count)])]
    ppermute x5 -> x6, starting transfers between devices: 4.87 us -> 6.49 us  [hop(): return lax.ppermute(x, 'ev', [(i, i ^ bit) for i in range(ev_count)])]
    ppermute x3, waiting for transfers between devices: 12 us -> 12.9 us  [swap(): return lax.ppermute(x, 'st', [(0, 1), (1, 0)])]
  transfers between devices with their start and end apart: 9 -> 10, of which waited for: 6 -> 6; matrix products, arithmetic and copies ran while one was open for 0% -> 0% of each run, Pallas kernels for 11% -> 11%
where the time goes in v3:
time: 64.1 us; the launch traced here: 63.7 us
  waiting for transfers between devices  35.4 us (55%)
  starting transfers between devices  17.6 us (27%)
  Pallas kernels  10.6 us (17%)
    ppermute x6, waiting for transfers between devices, hop(): return lax.ppermute(x, 'ev', [(i, i ^ bit) for i in range(ev_count)])  22.5 us
    ppermute x3, waiting for transfers between devices, swap(): return lax.ppermute(x, 'st', [(0, 1), (1, 0)])  12.9 us
    all_to_all x1, starting transfers between devices, paired_steps(): moved = lax.all_to_all(pieces, 'ev', 0, 0, tiled=True)  7.43 us
    ppermute x6, starting transfers between devices, hop(): return lax.ppermute(x, 'ev', [(i, i ^ bit) for i in range(ev_count)])  6.49 us
    ppermute x3, starting transfers between devices, swap(): return lax.ppermute(x, 'st', [(0, 1), (1, 0)])  3.65 us
    pallas_call x2, Pallas kernels, held(): pl.pallas_call(held_kernel, out_shape=(part, part, jax.ShapeDtypeStruct((...  3.25 us
    pallas_call x1, Pallas kernels, first_pieces(): pl.pallas_call(functools.partial(first_kernel, st_count), out_shape=(jax....  2.77 us
    pallas_call x1, Pallas kernels, green_pieces(): pl.pallas_call(green_kernel, out_shape=jax.ShapeDtypeStruct(shape, green....  1.86 us
  transfers between devices with their start and end apart: 10, of which 6 were waited for; matrix products, arithmetic and copies ran while one was open for 0% of the time, Pallas kernels for 11%

profile of v3, /device:TPU:0, one launch (start us, length us, event | category | flops | bytes accessed | tf_op | source)
XLA Modules:
  0.0 63.7 jit_solution(15681793878582453692)
XLA Ops:
  0.0 2.8 %first_pieces.1 = (bf16[6,3,128,128]{3,2,1,0:T(8,128)(2,1)}, bf16[2,3,16,128]{3,2,1,0:T(8,128)(2,1)S(1)}, bf16[16,12,16,128]{3,2,1,0:T(8,128)(2,1)}) custom-call(s32[1]{0:T(128)} %bitcast.1.side_ref, bf16[6,6,128,256]{3,2,1,0:T(8,128)(2,1)} %bitcast.14, bf16[2,3,16,128]{3,2,1,0:T(8,128)(2,1)} %weights_ref.1, s32[16,128]{1,0:T(8,128)} %mask_ref.1, ...), custom_call_target="tpu_custom_call" | custom-call | tf_op jit(solution)/shard_map/first_pieces/pallas_call | solution.py:126
  2.8 7.4 %all-to-all-start = ((bf16[16,12,16,128]{3,2,1,0:T(8,128)(2,1)}), bf16[16,12,16,128]{3,2,1,0:T(8,128)(2,1)S(1)}, u32[]{:S(2)}, u32[]{:S(2)}) async-start(bf16[16,12,16,128]{3,2,1,0:T(8,128)(2,1)} %get-tuple-element.14), calls=%async_computation | async-start | bytes 1572864 | tf_op jit(solution)/shard_map/all_to_all | solution.py:377
  10.2 1.9 %collective-permute-start = (bf16[2,3,16,128]{3,2,1,0:T(8,128)(2,1)S(1)}, bf16[2,3,16,128]{3,2,1,0:T(8,128)(2,1)S(1)}, u32[]{:S(2)}, u32[]{:S(2)}) collective-permute-start(bf16[2,3,16,128]{3,2,1,0:T(8,128)(2,1)S(1)} %get-tuple-element.15), channel_id=1, source_target_pairs={{0,8},{2,10},{4,12},{6,14},{8,0},{10,2},{12,4},{14,6},{16,24},{18,... | collective-permute-start | bytes 73736 | tf_op jit(solution)/shard_map/ppermute | solution.py:366
  12.1 2.4 %collective-permute-start.1 = (bf16[2,3,16,128]{3,2,1,0:T(8,128)(2,1)S(1)}, bf16[2,3,16,128]{3,2,1,0:T(8,128)(2,1)S(1)}, u32[]{:S(2)}, u32[]{:S(2)}) collective-permute-start(bf16[2,3,16,128]{3,2,1,0:T(8,128)(2,1)S(1)} %get-tuple-element.15), channel_id=1, source_target_pairs={{0,16},{2,18},{4,20},{6,22},{8,24},{10,26},{12,28},{14,30},{16,0},... | collective-permute-start | bytes 73736 | tf_op jit(solution)/shard_map/ppermute | solution.py:366
  14.5 0.2 collective-permute-start.2
  14.7 10.0 %collective-permute-done = bf16[2,3,16,128]{3,2,1,0:T(8,128)(2,1)S(1)} collective-permute-done((bf16[2,3,16,128]{3,2,1,0:T(8,128)(2,1)S(1)}, bf16[2,3,16,128]{3,2,1,0:T(8,128)(2,1)S(1)}, u32[]{:S(2)}, u32[]{:S(2)}) %collective-permute-start) | collective-permute-done | bytes 24608 | tf_op jit(solution)/shard_map/ppermute | solution.py:366
  24.7 8.3 %collective-permute-done.1 = bf16[2,3,16,128]{3,2,1,0:T(8,128)(2,1)S(1)} collective-permute-done((bf16[2,3,16,128]{3,2,1,0:T(8,128)(2,1)S(1)}, bf16[2,3,16,128]{3,2,1,0:T(8,128)(2,1)S(1)}, u32[]{:S(2)}, u32[]{:S(2)}) %collective-permute-start.1) | collective-permute-done | bytes 24608 | tf_op jit(solution)/shard_map/ppermute | solution.py:366
  33.0 1.6 %collective-permute-start.3 = (bf16[4,2,3,16,128]{4,3,2,1,0:T(8,128)(2,1)S(1)}, bf16[4,2,3,16,128]{4,3,2,1,0:T(8,128)(2,1)S(1)}, u32[]{:S(2)}, u32[]{:S(2)}) collective-permute-start(bf16[4,2,3,16,128]{4,3,2,1,0:T(8,128)(2,1)S(1)} %get-tuple-element.24), channel_id=1, source_target_pairs={{0,1},{1,0},{2,3},{3,2},{4,5},{5,4},{6,7},{7,6},{8,9},{9,8},{10,11... | collective-permute-start | bytes 294920 | tf_op jit(solution)/shard_map/ppermute | solution.py:369
  34.5 0.5 collective-permute-start.5
  35.1 1.9 %green_pieces.1 = bf16[6,3,128,128]{3,2,1,0:T(8,128)(2,1)} custom-call(s32[1]{0:T(128)} %bitcast.1.side_ref, bf16[6,6,128,256]{3,2,1,0:T(8,128)(2,1)} %bitcast.15), custom_call_target="tpu_custom_call" | custom-call | tf_op jit(solution)/shard_map/green_pieces/pallas_call | solution.py:166
  36.9 1.6 %collective-permute-start.8 = (bf16[6,3,128,128]{3,2,1,0:T(8,128)(2,1)}, bf16[6,3,128,128]{3,2,1,0:T(8,128)(2,1)S(1)}, u32[]{:S(2)}, u32[]{:S(2)}) collective-permute-start(bf16[6,3,128,128]{3,2,1,0:T(8,128)(2,1)} %green_pieces.1), channel_id=1, source_target_pairs={{0,1},{1,0},{2,3},{3,2},{4,5},{5,4},{6,7},{7,6},{8,9},{9,8},{10,11... | collective-permute-start | bytes 1769480 | tf_op jit(solution)/shard_map/ppermute | solution.py:369
  38.5 0.2 collective-permute-done.3
  38.7 1.5 %collective-permute-start.6 = (bf16[2,4,2,3,16,128]{5,4,3,2,1,0:T(8,128)(2,1)S(1)}, bf16[2,4,2,3,16,128]{5,4,3,2,1,0:T(8,128)(2,1)S(1)}, u32[]{:S(2)}, u32[]{:S(2)}) collective-permute-start(bf16[2,4,2,3,16,128]{5,4,3,2,1,0:T(8,128)(2,1)S(1)} %pad_maximum_fusion.near_ref), channel_id=1, source_target_pairs={{0,4},{2,6},{4,0},{6,2},{8,12},{10,14},{12,8},{14,10},{16,20},{18,... | collective-permute-start | bytes 589832 | tf_op jit(solution)/shard_map/ppermute | solution.py:366
  40.3 4.2 %collective-permute-done.6.near_ref = bf16[2,4,2,3,16,128]{5,4,3,2,1,0:T(8,128)(2,1)S(1)} collective-permute-done((bf16[2,4,2,3,16,128]{5,4,3,2,1,0:T(8,128)(2,1)S(1)}, bf16[2,4,2,3,16,128]{5,4,3,2,1,0:T(8,128)(2,1)S(1)}, u32[]{:S(2)}, u32[]{:S(2)}) %collective-permute-start.6) | collective-permute-done | bytes 196640 | tf_op jit(solution)/shard_map/ppermute | solution.py:366
  44.5 0.0 collective-permute-start.7
  44.5 0.5 collective-permute-start.4
  45.0 1.4 %own_green.1.own_ref = bf16[6,6,128,128]{3,2,1,0:T(8,128)(2,1)S(1)} custom-call(s32[1]{0:T(128)} %bitcast.1.side_ref, bf16[6,6,128,256]{3,2,1,0:T(8,128)(2,1)} %bitcast.16), custom_call_target="tpu_custom_call" | custom-call | tf_op jit(solution)/shard_map/own_green/pallas_call | solution.py:195
  46.4 5.0 %collective-permute-done.5.other_ref = bf16[6,3,128,128]{3,2,1,0:T(8,128)(2,1)S(1)} collective-permute-done((bf16[6,3,128,128]{3,2,1,0:T(8,128)(2,1)}, bf16[6,3,128,128]{3,2,1,0:T(8,128)(2,1)S(1)}, u32[]{:S(2)}, u32[]{:S(2)}) %collective-permute-start.5) | collective-permute-done | bytes 589856 | tf_op jit(solution)/shard_map/ppermute | solution.py:369
  51.4 1.6 %shard_map.47 = (f32[256,384]{1,0:T(8,128)S(1)}, f32[256,384]{1,0:T(8,128)S(1)}, bf16[128,768]{1,0:T(8,128)(2,1)S(1)}) custom-call(bf16[2,4,2,3,16,128]{5,4,3,2,1,0:T(8,128)(2,1)S(1)} %collective-permute-done.6.near_ref, bf16[2,4,2,3,16,128]{5,4,3,2,1,0:T(8,128)(2,1)} %collective-permute-done.7.core_ref, bf16[6,6,128,128]{3,2,1,0:T(8,128)(2,1)S(1)} %own_green.1.own_ref, ...), custom_call_target="tpu_custom_call" | custom-call | tf_op jit(solution)/shard_map/pallas_call | solution.py:265
  53.0 0.0 collective-permute-done.4.core_ref
  53.0 1.6 %shard_map.46 = (f32[256,384]{1,0:T(8,128)S(1)}, f32[256,384]{1,0:T(8,128)S(1)}, bf16[128,768]{1,0:T(8,128)(2,1)S(1)}) custom-call(bf16[2,4,2,3,16,128]{5,4,3,2,1,0:T(8,128)(2,1)S(1)} %pad_maximum_fusion.near_ref, bf16[2,4,2,3,16,128]{5,4,3,2,1,0:T(8,128)(2,1)} %collective-permute-done.4.core_ref, bf16[6,6,128,128]{3,2,1,0:T(8,128)(2,1)S(1)} %own_green.1.own_ref, ...), custom_call_target="tpu_custom_call" | custom-call | tf_op jit(solution)/shard_map/pallas_call | solution.py:265
  54.6 7.7 %collective-permute-done.8.other_ref = bf16[6,3,128,128]{3,2,1,0:T(8,128)(2,1)S(1)} collective-permute-done((bf16[6,3,128,128]{3,2,1,0:T(8,128)(2,1)}, bf16[6,3,128,128]{3,2,1,0:T(8,128)(2,1)S(1)}, u32[]{:S(2)}, u32[]{:S(2)}) %collective-permute-start.8) | collective-permute-done | bytes 589856 | tf_op jit(solution)/shard_map/ppermute | solution.py:369
  62.4 0.6 held_rest.1.full_ref
  63.0 0.8 %combine.1 = f32[2,128]{1,0:T(2,128)} custom-call(s32[1]{0:T(128)} %bitcast.me_ref, bf16[16,12,16,128]{3,2,1,0:T(8,128)(2,1)S(1)} %all-to-all-done.strain_ref, f32[2,256,768]{2,1,0:T(8,128)S(1)} %held_rest.1.full_ref), custom_call_target="tpu_custom_call" | custom-call | tf_op jit(solution)/shard_map/combine/pallas_call | solution.py:343
  (5 shorter events, 0.0 us)
Async XLA Ops:
  2.8 60.2 %all-to-all-start = ((bf16[16,12,16,128]{3,2,1,0:T(8,128)(2,1)}), bf16[16,12,16,128]{3,2,1,0:T(8,128)(2,1)S(1)}, u32[]{:S(2)}, u32[]{:S(2)}) async-start(bf16[16,12,16,128]{3,2,1,0:T(8,128)(2,1)} %get-tuple-element.14), calls=%async_computation | async-start | bytes 1572864 | tf_op jit(solution)/shard_map/all_to_all | solution.py:377
  10.2 14.4 %collective-permute-start = (bf16[2,3,16,128]{3,2,1,0:T(8,128)(2,1)S(1)}, bf16[2,3,16,128]{3,2,1,0:T(8,128)(2,1)S(1)}, u32[]{:S(2)}, u32[]{:S(2)}) collective-permute-start(bf16[2,3,16,128]{3,2,1,0:T(8,128)(2,1)S(1)} %get-tuple-element.15), channel_id=1, source_target_pairs={{0,8},{2,10},{4,12},{6,14},{8,0},{10,2},{12,4},{14,6},{16,24},{18,... | collective-permute-start | bytes 73736 | tf_op jit(solution)/shard_map/ppermute | solution.py:366
  12.1 20.8 %collective-permute-start.1 = (bf16[2,3,16,128]{3,2,1,0:T(8,128)(2,1)S(1)}, bf16[2,3,16,128]{3,2,1,0:T(8,128)(2,1)S(1)}, u32[]{:S(2)}, u32[]{:S(2)}) collective-permute-start(bf16[2,3,16,128]{3,2,1,0:T(8,128)(2,1)S(1)} %get-tuple-element.15), channel_id=1, source_target_pairs={{0,16},{2,18},{4,20},{6,22},{8,24},{10,26},{12,28},{14,30},{16,0},... | collective-permute-start | bytes 73736 | tf_op jit(solution)/shard_map/ppermute | solution.py:366
  14.5 18.4 %collective-permute-start.2 = (bf16[2,3,16,128]{3,2,1,0:T(8,128)(2,1)S(1)}, bf16[2,3,16,128]{3,2,1,0:T(8,128)(2,1)S(1)}, u32[]{:S(2)}, u32[]{:S(2)}) collective-permute-start(bf16[2,3,16,128]{3,2,1,0:T(8,128)(2,1)S(1)} %get-tuple-element.15), channel_id=1, source_target_pairs={{0,24},{2,26},{4,28},{6,30},{8,16},{10,18},{12,20},{14,22},{16,8},... | collective-permute-start | bytes 73736 | tf_op jit(solution)/shard_map/ppermute | solution.py:366
  33.0 5.7 %collective-permute-start.3 = (bf16[4,2,3,16,128]{4,3,2,1,0:T(8,128)(2,1)S(1)}, bf16[4,2,3,16,128]{4,3,2,1,0:T(8,128)(2,1)S(1)}, u32[]{:S(2)}, u32[]{:S(2)}) collective-permute-start(bf16[4,2,3,16,128]{4,3,2,1,0:T(8,128)(2,1)S(1)} %get-tuple-element.24), channel_id=1, source_target_pairs={{0,1},{1,0},{2,3},{3,2},{4,5},{5,4},{6,7},{7,6},{8,9},{9,8},{10,11... | collective-permute-start | bytes 294920 | tf_op jit(solution)/shard_map/ppermute | solution.py:369
  34.5 16.8 %collective-permute-start.5 = (bf16[6,3,128,128]{3,2,1,0:T(8,128)(2,1)}, bf16[6,3,128,128]{3,2,1,0:T(8,128)(2,1)S(1)}, u32[]{:S(2)}, u32[]{:S(2)}) collective-permute-start(bf16[6,3,128,128]{3,2,1,0:T(8,128)(2,1)} %get-tuple-element.16), channel_id=1, source_target_pairs={{0,1},{1,0},{2,3},{3,2},{4,5},{5,4},{6,7},{7,6},{8,9},{9,8},{10,11... | collective-permute-start | bytes 1769480 | tf_op jit(solution)/shard_map/ppermute | solution.py:369
  36.9 25.4 %collective-permute-start.8 = (bf16[6,3,128,128]{3,2,1,0:T(8,128)(2,1)}, bf16[6,3,128,128]{3,2,1,0:T(8,128)(2,1)S(1)}, u32[]{:S(2)}, u32[]{:S(2)}) collective-permute-start(bf16[6,3,128,128]{3,2,1,0:T(8,128)(2,1)} %green_pieces.1), channel_id=1, source_target_pairs={{0,1},{1,0},{2,3},{3,2},{4,5},{5,4},{6,7},{7,6},{8,9},{9,8},{10,11... | collective-permute-start | bytes 1769480 | tf_op jit(solution)/shard_map/ppermute | solution.py:369
  38.7 5.7 %collective-permute-start.6 = (bf16[2,4,2,3,16,128]{5,4,3,2,1,0:T(8,128)(2,1)S(1)}, bf16[2,4,2,3,16,128]{5,4,3,2,1,0:T(8,128)(2,1)S(1)}, u32[]{:S(2)}, u32[]{:S(2)}) collective-permute-start(bf16[2,4,2,3,16,128]{5,4,3,2,1,0:T(8,128)(2,1)S(1)} %pad_maximum_fusion.near_ref), channel_id=1, source_target_pairs={{0,4},{2,6},{4,0},{6,2},{8,12},{10,14},{12,8},{14,10},{16,20},{18,... | collective-permute-start | bytes 589832 | tf_op jit(solution)/shard_map/ppermute | solution.py:366
  44.5 1.9 %collective-permute-start.7 = (bf16[2,4,2,3,16,128]{5,4,3,2,1,0:T(8,128)(2,1)S(1)}, bf16[2,4,2,3,16,128]{5,4,3,2,1,0:T(8,128)(2,1)}, u32[]{:S(2)}, u32[]{:S(2)}) collective-permute-start(bf16[2,4,2,3,16,128]{5,4,3,2,1,0:T(8,128)(2,1)S(1)} %collective-permute-done.6.near_ref), channel_id=1, source_target_pairs={{0,2},{2,0},{4,6},{6,4},{8,10},{10,8},{12,14},{14,12},{16,18},{18,... | collective-permute-start | bytes 589832 | tf_op jit(solution)/shard_map/ppermute | solution.py:366
  44.5 8.5 %collective-permute-start.4 = (bf16[2,4,2,3,16,128]{5,4,3,2,1,0:T(8,128)(2,1)S(1)}, bf16[2,4,2,3,16,128]{5,4,3,2,1,0:T(8,128)(2,1)}, u32[]{:S(2)}, u32[]{:S(2)}) collective-permute-start(bf16[2,4,2,3,16,128]{5,4,3,2,1,0:T(8,128)(2,1)S(1)} %pad_maximum_fusion.near_ref), channel_id=1, source_target_pairs={{0,2},{2,0},{4,6},{6,4},{8,10},{10,8},{12,14},{14,12},{16,18},{18,... | collective-permute-start | bytes 589832 | tf_op jit(solution)/shard_map/ppermute | solution.py:366

commit v4 on v3

--- a/solution.py
+++ b/solution.py
@@ -103,17 +103,21 @@
             )
         )
         gives.append(pltpu.make_async_copy(pieces_buf.at[i], pieces_ref.at[i], pieces_sems.at[i]))
-    for copy in small + takes:
+    count = sems.shape[0]
+    priorities = [0] * count + [1] * (len(takes) - count)
+    for copy in small:
         copy.start()
+    for copy, priority in zip(takes, priorities):
+        copy.start(priority=priority)
     for copy in small:
         copy.wait()
     keep = mask_buf[...].astype(jnp.bfloat16)
     for r in range(2):
         for f in range(3):
             masked_ref[r, f] = weights_buf[r, f] * keep
-    for take, give in zip(takes, gives):
+    for take, give, priority in zip(takes, gives, priorities):
         take.wait()
-        give.start()
+        give.start(priority=priority)
     for copy in gives:
         copy.wait()
 
@@ -376,10 +380,11 @@
     gathered = jnp.stack([masked] + [hop(masked, bit) for bit in range(4, ev_count, 4)])
     moved = lax.all_to_all(pieces, "ev", 0, 0, tiled=True)
 
-    near = jnp.stack([gathered, swap(gathered)])
+    partner = swap(gathered)
+    near = jnp.stack([gathered, partner])
     sent_rest = green_pieces(side, green)
     other_rest = swap(sent_rest)
-    y = hop(near, 2)
+    y = jnp.stack([hop(gathered, 2), hop(partner, 2)])
     core = hop(near, 1)
     both = hop(y, 1)
 

time: 64.1 us -> 63.8 us (level)
    ppermute x6 -> x7, starting transfers between devices: 6.49 us -> 7.11 us  [hop(): return lax.ppermute(x, 'ev', [(i, i ^ bit) for i in range(ev_count)])]
    ppermute x6 -> x7, waiting for transfers between devices: 22.5 us -> 22.3 us  [hop(): return lax.ppermute(x, 'ev', [(i, i ^ bit) for i in range(ev_count)])]
  transfers between devices with their start and end apart: 10 -> 11, of which waited for: 6 -> 6; matrix products, arithmetic and copies ran while one was open for 0% -> 0% of each run, Pallas kernels for 11% -> 11%
where the time goes in v4:
time: 63.8 us; the launch traced here: 63.5 us
  waiting for transfers between devices  34.8 us (55%)
  starting transfers between devices  18.2 us (29%)
  Pallas kernels  10.4 us (16%)
    ppermute x7, waiting for transfers between devices, hop(): return lax.ppermute(x, 'ev', [(i, i ^ bit) for i in range(ev_count)])  22.3 us
    ppermute x3, waiting for transfers between devices, swap(): return lax.ppermute(x, 'st', [(0, 1), (1, 0)])  12.4 us
    all_to_all x1, starting transfers between devices, paired_steps(): moved = lax.all_to_all(pieces, 'ev', 0, 0, tiled=True)  7.43 us
    ppermute x7, starting transfers between devices, hop(): return lax.ppermute(x, 'ev', [(i, i ^ bit) for i in range(ev_count)])  7.11 us
    ppermute x3, starting transfers between devices, swap(): return lax.ppermute(x, 'st', [(0, 1), (1, 0)])  3.65 us
    pallas_call x2, Pallas kernels, held(): pl.pallas_call(held_kernel, out_shape=(part, part, jax.ShapeDtypeStruct((...  3.25 us
    pallas_call x1, Pallas kernels, first_pieces(): pl.pallas_call(functools.partial(first_kernel, st_count), out_shape=(jax....  2.5 us
    pallas_call x1, Pallas kernels, green_pieces(): pl.pallas_call(green_kernel, out_shape=jax.ShapeDtypeStruct(shape, green....  1.87 us
  transfers between devices with their start and end apart: 11, of which 6 were waited for; matrix products, arithmetic and copies ran while one was open for 0% of the time, Pallas kernels for 11%

profile of v4, /device:TPU:0, one launch (start us, length us, event | category | flops | bytes accessed | tf_op | source)
XLA Modules:
  0.0 63.5 jit_solution(5165548712624674064)
XLA Ops:
  0.0 2.5 %first_pieces.1 = (bf16[6,3,128,128]{3,2,1,0:T(8,128)(2,1)}, bf16[2,3,16,128]{3,2,1,0:T(8,128)(2,1)S(1)}, bf16[16,12,16,128]{3,2,1,0:T(8,128)(2,1)}) custom-call(s32[1]{0:T(128)} %bitcast.1.side_ref, bf16[6,6,128,256]{3,2,1,0:T(8,128)(2,1)} %bitcast.16, bf16[2,3,16,128]{3,2,1,0:T(8,128)(2,1)} %weights_ref.1, s32[16,128]{1,0:T(8,128)} %mask_ref.1, ...), custom_call_target="tpu_custom_call" | custom-call | tf_op jit(solution)/shard_map/first_pieces/pallas_call | solution.py:130
  2.5 7.4 %all-to-all-start = ((bf16[16,12,16,128]{3,2,1,0:T(8,128)(2,1)}), bf16[16,12,16,128]{3,2,1,0:T(8,128)(2,1)S(1)}, u32[]{:S(2)}, u32[]{:S(2)}) async-start(bf16[16,12,16,128]{3,2,1,0:T(8,128)(2,1)} %get-tuple-element.14), calls=%async_computation | async-start | bytes 1572864 | tf_op jit(solution)/shard_map/all_to_all | solution.py:381
  9.9 1.9 %collective-permute-start = (bf16[2,3,16,128]{3,2,1,0:T(8,128)(2,1)S(1)}, bf16[2,3,16,128]{3,2,1,0:T(8,128)(2,1)S(1)}, u32[]{:S(2)}, u32[]{:S(2)}) collective-permute-start(bf16[2,3,16,128]{3,2,1,0:T(8,128)(2,1)S(1)} %get-tuple-element.15), channel_id=1, source_target_pairs={{0,8},{2,10},{4,12},{6,14},{8,0},{10,2},{12,4},{14,6},{16,24},{18,... | collective-permute-start | bytes 73736 | tf_op jit(solution)/shard_map/ppermute | solution.py:370
  11.9 2.4 %collective-permute-start.1 = (bf16[2,3,16,128]{3,2,1,0:T(8,128)(2,1)S(1)}, bf16[2,3,16,128]{3,2,1,0:T(8,128)(2,1)S(1)}, u32[]{:S(2)}, u32[]{:S(2)}) collective-permute-start(bf16[2,3,16,128]{3,2,1,0:T(8,128)(2,1)S(1)} %get-tuple-element.15), channel_id=1, source_target_pairs={{0,16},{2,18},{4,20},{6,22},{8,24},{10,26},{12,28},{14,30},{16,0},... | collective-permute-start | bytes 73736 | tf_op jit(solution)/shard_map/ppermute | solution.py:370
  14.2 0.2 collective-permute-start.2
  14.4 10.0 %collective-permute-done = bf16[2,3,16,128]{3,2,1,0:T(8,128)(2,1)S(1)} collective-permute-done((bf16[2,3,16,128]{3,2,1,0:T(8,128)(2,1)S(1)}, bf16[2,3,16,128]{3,2,1,0:T(8,128)(2,1)S(1)}, u32[]{:S(2)}, u32[]{:S(2)}) %collective-permute-start) | collective-permute-done | bytes 24608 | tf_op jit(solution)/shard_map/ppermute | solution.py:370
  24.4 8.3 %collective-permute-done.1 = bf16[2,3,16,128]{3,2,1,0:T(8,128)(2,1)S(1)} collective-permute-done((bf16[2,3,16,128]{3,2,1,0:T(8,128)(2,1)S(1)}, bf16[2,3,16,128]{3,2,1,0:T(8,128)(2,1)S(1)}, u32[]{:S(2)}, u32[]{:S(2)}) %collective-permute-start.1) | collective-permute-done | bytes 24608 | tf_op jit(solution)/shard_map/ppermute | solution.py:370
  32.7 1.6 %collective-permute-start.3 = (bf16[4,2,3,16,128]{4,3,2,1,0:T(8,128)(2,1)S(1)}, bf16[4,2,3,16,128]{4,3,2,1,0:T(8,128)(2,1)S(1)}, u32[]{:S(2)}, u32[]{:S(2)}) collective-permute-start(bf16[4,2,3,16,128]{4,3,2,1,0:T(8,128)(2,1)S(1)} %get-tuple-element.24), channel_id=1, source_target_pairs={{0,1},{1,0},{2,3},{3,2},{4,5},{5,4},{6,7},{7,6},{8,9},{9,8},{10,11... | collective-permute-start | bytes 294920 | tf_op jit(solution)/shard_map/ppermute | solution.py:373
  34.3 0.5 collective-permute-start.5
  34.8 1.9 %green_pieces.1 = bf16[6,3,128,128]{3,2,1,0:T(8,128)(2,1)} custom-call(s32[1]{0:T(128)} %bitcast.1.side_ref, bf16[6,6,128,256]{3,2,1,0:T(8,128)(2,1)} %bitcast.17), custom_call_target="tpu_custom_call" | custom-call | tf_op jit(solution)/shard_map/green_pieces/pallas_call | solution.py:170
  36.7 1.6 %collective-permute-start.9 = (bf16[6,3,128,128]{3,2,1,0:T(8,128)(2,1)}, bf16[6,3,128,128]{3,2,1,0:T(8,128)(2,1)S(1)}, u32[]{:S(2)}, u32[]{:S(2)}) collective-permute-start(bf16[6,3,128,128]{3,2,1,0:T(8,128)(2,1)} %green_pieces.1), channel_id=1, source_target_pairs={{0,1},{1,0},{2,3},{3,2},{4,5},{5,4},{6,7},{7,6},{8,9},{9,8},{10,11... | collective-permute-start | bytes 1769480 | tf_op jit(solution)/shard_map/ppermute | solution.py:373
  38.2 1.5 %collective-permute-start.6 = (bf16[4,2,3,16,128]{4,3,2,1,0:T(8,128)(2,1)S(1)}, bf16[4,2,3,16,128]{4,3,2,1,0:T(8,128)(2,1)S(1)}, u32[]{:S(2)}, u32[]{:S(2)}) collective-permute-start(bf16[4,2,3,16,128]{4,3,2,1,0:T(8,128)(2,1)S(1)} %get-tuple-element.24), channel_id=1, source_target_pairs={{0,4},{2,6},{4,0},{6,2},{8,12},{10,14},{12,8},{14,10},{16,20},{18,... | collective-permute-start | bytes 294920 | tf_op jit(solution)/shard_map/ppermute | solution.py:370
  39.7 0.6 collective-permute-start.7
  40.3 2.6 %collective-permute-done.6 = bf16[4,2,3,16,128]{4,3,2,1,0:T(8,128)(2,1)S(1)} collective-permute-done((bf16[4,2,3,16,128]{4,3,2,1,0:T(8,128)(2,1)S(1)}, bf16[4,2,3,16,128]{4,3,2,1,0:T(8,128)(2,1)S(1)}, u32[]{:S(2)}, u32[]{:S(2)}) %collective-permute-start.6) | collective-permute-done | bytes 98336 | tf_op jit(solution)/shard_map/ppermute | solution.py:370
  42.9 1.5 %collective-permute-done.7 = bf16[4,2,3,16,128]{4,3,2,1,0:T(8,128)(2,1)S(1)} collective-permute-done((bf16[4,2,3,16,128]{4,3,2,1,0:T(8,128)(2,1)S(1)}, bf16[4,2,3,16,128]{4,3,2,1,0:T(8,128)(2,1)S(1)}, u32[]{:S(2)}, u32[]{:S(2)}) %collective-permute-start.7) | collective-permute-done | bytes 98336 | tf_op jit(solution)/shard_map/ppermute | solution.py:370
  44.4 0.1 collective-permute-start.8
  44.5 0.6 collective-permute-start.4
  45.0 1.4 %own_green.1.own_ref = bf16[6,6,128,128]{3,2,1,0:T(8,128)(2,1)S(1)} custom-call(s32[1]{0:T(128)} %bitcast.1.side_ref, bf16[6,6,128,256]{3,2,1,0:T(8,128)(2,1)} %bitcast.18), custom_call_target="tpu_custom_call" | custom-call | tf_op jit(solution)/shard_map/own_green/pallas_call | solution.py:199
  46.4 4.7 %collective-permute-done.5.other_ref = bf16[6,3,128,128]{3,2,1,0:T(8,128)(2,1)S(1)} collective-permute-done((bf16[6,3,128,128]{3,2,1,0:T(8,128)(2,1)}, bf16[6,3,128,128]{3,2,1,0:T(8,128)(2,1)S(1)}, u32[]{:S(2)}, u32[]{:S(2)}) %collective-permute-start.5) | collective-permute-done | bytes 589856 | tf_op jit(solution)/shard_map/ppermute | solution.py:373
  51.1 1.6 %shard_map.47 = (f32[256,384]{1,0:T(8,128)S(1)}, f32[256,384]{1,0:T(8,128)S(1)}, bf16[128,768]{1,0:T(8,128)(2,1)S(1)}) custom-call(bf16[2,4,2,3,16,128]{5,4,3,2,1,0:T(8,128)(2,1)S(1)} %pad_maximum_fusion.1.near_ref, bf16[2,4,2,3,16,128]{5,4,3,2,1,0:T(8,128)(2,1)} %collective-permute-done.8.core_ref, bf16[6,6,128,128]{3,2,1,0:T(8,128)(2,1)S(1)} %own_green.1.own_ref, ...), custom_call_target="tpu_custom_call" | custom-call | tf_op jit(solution)/shard_map/pallas_call | solution.py:269
  52.7 1.6 %shard_map.46 = (f32[256,384]{1,0:T(8,128)S(1)}, f32[256,384]{1,0:T(8,128)S(1)}, bf16[128,768]{1,0:T(8,128)(2,1)S(1)}) custom-call(bf16[2,4,2,3,16,128]{5,4,3,2,1,0:T(8,128)(2,1)S(1)} %pad_maximum_fusion.near_ref, bf16[2,4,2,3,16,128]{5,4,3,2,1,0:T(8,128)(2,1)} %collective-permute-done.4.core_ref, bf16[6,6,128,128]{3,2,1,0:T(8,128)(2,1)S(1)} %own_green.1.own_ref, ...), custom_call_target="tpu_custom_call" | custom-call | tf_op jit(solution)/shard_map/pallas_call | solution.py:269
  54.4 7.7 %collective-permute-done.9.other_ref = bf16[6,3,128,128]{3,2,1,0:T(8,128)(2,1)S(1)} collective-permute-done((bf16[6,3,128,128]{3,2,1,0:T(8,128)(2,1)}, bf16[6,3,128,128]{3,2,1,0:T(8,128)(2,1)S(1)}, u32[]{:S(2)}, u32[]{:S(2)}) %collective-permute-start.9) | collective-permute-done | bytes 589856 | tf_op jit(solution)/shard_map/ppermute | solution.py:373
  62.1 0.6 held_rest.1.full_ref
  62.7 0.8 %combine.1 = f32[2,128]{1,0:T(2,128)} custom-call(s32[1]{0:T(128)} %bitcast.me_ref, bf16[16,12,16,128]{3,2,1,0:T(8,128)(2,1)S(1)} %all-to-all-done.strain_ref, f32[2,256,768]{2,1,0:T(8,128)S(1)} %held_rest.1.full_ref), custom_call_target="tpu_custom_call" | custom-call | tf_op jit(solution)/shard_map/combine/pallas_call | solution.py:347
  (8 shorter events, 0.1 us)
Async XLA Ops:
  2.5 60.2 %all-to-all-start = ((bf16[16,12,16,128]{3,2,1,0:T(8,128)(2,1)}), bf16[16,12,16,128]{3,2,1,0:T(8,128)(2,1)S(1)}, u32[]{:S(2)}, u32[]{:S(2)}) async-start(bf16[16,12,16,128]{3,2,1,0:T(8,128)(2,1)} %get-tuple-element.14), calls=%async_computation | async-start | bytes 1572864 | tf_op jit(solution)/shard_map/all_to_all | solution.py:381
  9.9 14.4 %collective-permute-start = (bf16[2,3,16,128]{3,2,1,0:T(8,128)(2,1)S(1)}, bf16[2,3,16,128]{3,2,1,0:T(8,128)(2,1)S(1)}, u32[]{:S(2)}, u32[]{:S(2)}) collective-permute-start(bf16[2,3,16,128]{3,2,1,0:T(8,128)(2,1)S(1)} %get-tuple-element.15), channel_id=1, source_target_pairs={{0,8},{2,10},{4,12},{6,14},{8,0},{10,2},{12,4},{14,6},{16,24},{18,... | collective-permute-start | bytes 73736 | tf_op jit(solution)/shard_map/ppermute | solution.py:370
  11.9 20.8 %collective-permute-start.1 = (bf16[2,3,16,128]{3,2,1,0:T(8,128)(2,1)S(1)}, bf16[2,3,16,128]{3,2,1,0:T(8,128)(2,1)S(1)}, u32[]{:S(2)}, u32[]{:S(2)}) collective-permute-start(bf16[2,3,16,128]{3,2,1,0:T(8,128)(2,1)S(1)} %get-tuple-element.15), channel_id=1, source_target_pairs={{0,16},{2,18},{4,20},{6,22},{8,24},{10,26},{12,28},{14,30},{16,0},... | collective-permute-start | bytes 73736 | tf_op jit(solution)/shard_map/ppermute | solution.py:370
  14.2 18.4 %collective-permute-start.2 = (bf16[2,3,16,128]{3,2,1,0:T(8,128)(2,1)S(1)}, bf16[2,3,16,128]{3,2,1,0:T(8,128)(2,1)S(1)}, u32[]{:S(2)}, u32[]{:S(2)}) collective-permute-start(bf16[2,3,16,128]{3,2,1,0:T(8,128)(2,1)S(1)} %get-tuple-element.15), channel_id=1, source_target_pairs={{0,24},{2,26},{4,28},{6,30},{8,16},{10,18},{12,20},{14,22},{16,8},... | collective-permute-start | bytes 73736 | tf_op jit(solution)/shard_map/ppermute | solution.py:370
  32.7 7.0 %collective-permute-start.3 = (bf16[4,2,3,16,128]{4,3,2,1,0:T(8,128)(2,1)S(1)}, bf16[4,2,3,16,128]{4,3,2,1,0:T(8,128)(2,1)S(1)}, u32[]{:S(2)}, u32[]{:S(2)}) collective-permute-start(bf16[4,2,3,16,128]{4,3,2,1,0:T(8,128)(2,1)S(1)} %get-tuple-element.24), channel_id=1, source_target_pairs={{0,1},{1,0},{2,3},{3,2},{4,5},{5,4},{6,7},{7,6},{8,9},{9,8},{10,11... | collective-permute-start | bytes 294920 | tf_op jit(solution)/shard_map/ppermute | solution.py:373
  34.3 16.8 %collective-permute-start.5 = (bf16[6,3,128,128]{3,2,1,0:T(8,128)(2,1)}, bf16[6,3,128,128]{3,2,1,0:T(8,128)(2,1)S(1)}, u32[]{:S(2)}, u32[]{:S(2)}) collective-permute-start(bf16[6,3,128,128]{3,2,1,0:T(8,128)(2,1)} %get-tuple-element.16), channel_id=1, source_target_pairs={{0,1},{1,0},{2,3},{3,2},{4,5},{5,4},{6,7},{7,6},{8,9},{9,8},{10,11... | collective-permute-start | bytes 1769480 | tf_op jit(solution)/shard_map/ppermute | solution.py:373
  36.7 25.4 %collective-permute-start.9 = (bf16[6,3,128,128]{3,2,1,0:T(8,128)(2,1)}, bf16[6,3,128,128]{3,2,1,0:T(8,128)(2,1)S(1)}, u32[]{:S(2)}, u32[]{:S(2)}) collective-permute-start(bf16[6,3,128,128]{3,2,1,0:T(8,128)(2,1)} %green_pieces.1), channel_id=1, source_target_pairs={{0,1},{1,0},{2,3},{3,2},{4,5},{5,4},{6,7},{7,6},{8,9},{9,8},{10,11... | collective-permute-start | bytes 1769480 | tf_op jit(solution)/shard_map/ppermute | solution.py:373
  38.2 4.6 %collective-permute-start.6 = (bf16[4,2,3,16,128]{4,3,2,1,0:T(8,128)(2,1)S(1)}, bf16[4,2,3,16,128]{4,3,2,1,0:T(8,128)(2,1)S(1)}, u32[]{:S(2)}, u32[]{:S(2)}) collective-permute-start(bf16[4,2,3,16,128]{4,3,2,1,0:T(8,128)(2,1)S(1)} %get-tuple-element.24), channel_id=1, source_target_pairs={{0,4},{2,6},{4,0},{6,2},{8,12},{10,14},{12,8},{14,10},{16,20},{18,... | collective-permute-start | bytes 294920 | tf_op jit(solution)/shard_map/ppermute | solution.py:370
  39.7 4.6 %collective-permute-start.7 = (bf16[4,2,3,16,128]{4,3,2,1,0:T(8,128)(2,1)S(1)}, bf16[4,2,3,16,128]{4,3,2,1,0:T(8,128)(2,1)S(1)}, u32[]{:S(2)}, u32[]{:S(2)}) collective-permute-start(bf16[4,2,3,16,128]{4,3,2,1,0:T(8,128)(2,1)S(1)} %collective-permute-done.3), channel_id=1, source_target_pairs={{0,4},{2,6},{4,0},{6,2},{8,12},{10,14},{12,8},{14,10},{16,20},{18,... | collective-permute-start | bytes 294920 | tf_op jit(solution)/shard_map/ppermute | solution.py:370
  44.4 2.1 %collective-permute-start.8 = (bf16[2,4,2,3,16,128]{5,4,3,2,1,0:T(8,128)(2,1)S(1)}, bf16[2,4,2,3,16,128]{5,4,3,2,1,0:T(8,128)(2,1)}, u32[]{:S(2)}, u32[]{:S(2)}) collective-permute-start(bf16[2,4,2,3,16,128]{5,4,3,2,1,0:T(8,128)(2,1)S(1)} %pad_maximum_fusion.1.near_ref), channel_id=1, source_target_pairs={{0,2},{2,0},{4,6},{6,4},{8,10},{10,8},{12,14},{14,12},{16,18},{18,... | collective-permute-start | bytes 589832 | tf_op jit(solution)/shard_map/ppermute | solution.py:370
  44.5 8.3 %collective-permute-start.4 = (bf16[2,4,2,3,16,128]{5,4,3,2,1,0:T(8,128)(2,1)S(1)}, bf16[2,4,2,3,16,128]{5,4,3,2,1,0:T(8,128)(2,1)}, u32[]{:S(2)}, u32[]{:S(2)}) collective-permute-start(bf16[2,4,2,3,16,128]{5,4,3,2,1,0:T(8,128)(2,1)S(1)} %pad_maximum_fusion.near_ref), channel_id=1, source_target_pairs={{0,2},{2,0},{4,6},{6,4},{8,10},{10,8},{12,14},{14,12},{16,18},{18,... | collective-permute-start | bytes 589832 | tf_op jit(solution)/shard_map/ppermute | solution.py:370

commit v5 on v4

--- a/solution.py
+++ b/solution.py
@@ -278,17 +278,16 @@
 
 def rest_kernel(
     rows_a_ref, rows_b_ref, held_a_ref, held_b_ref, before_a_ref, before_b_ref, other_ref,
-    full_ref, left,
+    full_ref,
 ):
     half = rows_a_ref.shape[0]
     base = held_a_ref.shape[1]
+    left = jnp.concatenate([rows_a_ref[...], rows_b_ref[...]], axis=0)
     full_ref[0, :, :base] = held_a_ref[...]
     full_ref[1, :, :base] = held_b_ref[...]
-    left[:half] = rows_a_ref[...]
-    left[half:] = rows_b_ref[...]
     for c in range(COMPONENTS // 2):
         lanes = slice(c * LANES, (c + 1) * LANES)
-        fresh = product(left[...], turned(other_ref, c))
+        fresh = product(left, turned(other_ref, c))
         for y, before_ref in enumerate((before_a_ref, before_b_ref)):
             mine = slice(y * half, (y + 1) * half)
             out = slice(base + c * LANES, base + (c + 1) * LANES)
@@ -297,13 +296,12 @@
 
 
 def held_rest(rows_a, rows_b, held_a, held_b, before_a, before_b, other):
-    half, depth = rows_a.shape
+    half = rows_a.shape[0]
     return pl.pallas_call(
         rest_kernel,
         out_shape=jax.ShapeDtypeStruct((2, 2 * half, COMPONENTS * LANES), jnp.float32),
         in_specs=[in_vmem()] * 7,
         out_specs=in_vmem(),
-        scratch_shapes=[pltpu.VMEM((2 * half, depth), rows_a.dtype)],
         compiler_params=params(),
         name="held_rest",
     )(rows_a, rows_b, held_a, held_b, before_a, before_b, other)

time: 63.8 us -> 63.8 us (level)
  no operation moved by 1% of the time
where the time goes in v5:
time: 63.8 us; the launch traced here: 63.5 us
  waiting for transfers between devices  34.8 us (55%)
  starting transfers between devices  18.2 us (29%)
  Pallas kernels  10.4 us (16%)
    ppermute x7, waiting for transfers between devices, hop(): return lax.ppermute(x, 'ev', [(i, i ^ bit) for i in range(ev_count)])  22.3 us
    ppermute x3, waiting for transfers between devices, swap(): return lax.ppermute(x, 'st', [(0, 1), (1, 0)])  12.4 us
    all_to_all x1, starting transfers between devices, paired_steps(): moved = lax.all_to_all(pieces, 'ev', 0, 0, tiled=True)  7.43 us
    ppermute x7, starting transfers between devices, hop(): return lax.ppermute(x, 'ev', [(i, i ^ bit) for i in range(ev_count)])  7.11 us
    ppermute x3, starting transfers between devices, swap(): return lax.ppermute(x, 'st', [(0, 1), (1, 0)])  3.65 us
    pallas_call x2, Pallas kernels, held(): pl.pallas_call(held_kernel, out_shape=(part, part, jax.ShapeDtypeStruct((...  3.25 us
    pallas_call x1, Pallas kernels, first_pieces(): pl.pallas_call(functools.partial(first_kernel, st_count), out_shape=(jax....  2.5 us
    pallas_call x1, Pallas kernels, green_pieces(): pl.pallas_call(green_kernel, out_shape=jax.ShapeDtypeStruct(shape, green....  1.87 us
  transfers between devices with their start and end apart: 11, of which 6 were waited for; matrix products, arithmetic and copies ran while one was open for 0% of the time, Pallas kernels for 11%

profile of v5, /device:TPU:0, one launch (start us, length us, event | category | flops | bytes accessed | tf_op | source)
XLA Modules:
  0.0 63.5 jit_solution(5165548712624674064)
XLA Ops:
  0.0 2.5 %first_pieces.1 = (bf16[6,3,128,128]{3,2,1,0:T(8,128)(2,1)}, bf16[2,3,16,128]{3,2,1,0:T(8,128)(2,1)S(1)}, bf16[16,12,16,128]{3,2,1,0:T(8,128)(2,1)}) custom-call(s32[1]{0:T(128)} %bitcast.1.side_ref, bf16[6,6,128,256]{3,2,1,0:T(8,128)(2,1)} %bitcast.16, bf16[2,3,16,128]{3,2,1,0:T(8,128)(2,1)} %weights_ref.1, s32[16,128]{1,0:T(8,128)} %mask_ref.1, ...), custom_call_target="tpu_custom_call" | custom-call | tf_op jit(solution)/shard_map/first_pieces/pallas_call | solution.py:130
  2.5 7.4 %all-to-all-start = ((bf16[16,12,16,128]{3,2,1,0:T(8,128)(2,1)}), bf16[16,12,16,128]{3,2,1,0:T(8,128)(2,1)S(1)}, u32[]{:S(2)}, u32[]{:S(2)}) async-start(bf16[16,12,16,128]{3,2,1,0:T(8,128)(2,1)} %get-tuple-element.14), calls=%async_computation | async-start | bytes 1572864 | tf_op jit(solution)/shard_map/all_to_all | solution.py:379
  9.9 1.9 %collective-permute-start = (bf16[2,3,16,128]{3,2,1,0:T(8,128)(2,1)S(1)}, bf16[2,3,16,128]{3,2,1,0:T(8,128)(2,1)S(1)}, u32[]{:S(2)}, u32[]{:S(2)}) collective-permute-start(bf16[2,3,16,128]{3,2,1,0:T(8,128)(2,1)S(1)} %get-tuple-element.15), channel_id=1, source_target_pairs={{0,8},{2,10},{4,12},{6,14},{8,0},{10,2},{12,4},{14,6},{16,24},{18,... | collective-permute-start | bytes 73736 | tf_op jit(solution)/shard_map/ppermute | solution.py:368
  11.9 2.4 %collective-permute-start.1 = (bf16[2,3,16,128]{3,2,1,0:T(8,128)(2,1)S(1)}, bf16[2,3,16,128]{3,2,1,0:T(8,128)(2,1)S(1)}, u32[]{:S(2)}, u32[]{:S(2)}) collective-permute-start(bf16[2,3,16,128]{3,2,1,0:T(8,128)(2,1)S(1)} %get-tuple-element.15), channel_id=1, source_target_pairs={{0,16},{2,18},{4,20},{6,22},{8,24},{10,26},{12,28},{14,30},{16,0},... | collective-permute-start | bytes 73736 | tf_op jit(solution)/shard_map/ppermute | solution.py:368
  14.2 0.2 collective-permute-start.2
  14.4 10.0 %collective-permute-done = bf16[2,3,16,128]{3,2,1,0:T(8,128)(2,1)S(1)} collective-permute-done((bf16[2,3,16,128]{3,2,1,0:T(8,128)(2,1)S(1)}, bf16[2,3,16,128]{3,2,1,0:T(8,128)(2,1)S(1)}, u32[]{:S(2)}, u32[]{:S(2)}) %collective-permute-start) | collective-permute-done | bytes 24608 | tf_op jit(solution)/shard_map/ppermute | solution.py:368
  24.4 8.3 %collective-permute-done.1 = bf16[2,3,16,128]{3,2,1,0:T(8,128)(2,1)S(1)} collective-permute-done((bf16[2,3,16,128]{3,2,1,0:T(8,128)(2,1)S(1)}, bf16[2,3,16,128]{3,2,1,0:T(8,128)(2,1)S(1)}, u32[]{:S(2)}, u32[]{:S(2)}) %collective-permute-start.1) | collective-permute-done | bytes 24608 | tf_op jit(solution)/shard_map/ppermute | solution.py:368
  32.7 1.6 %collective-permute-start.3 = (bf16[4,2,3,16,128]{4,3,2,1,0:T(8,128)(2,1)S(1)}, bf16[4,2,3,16,128]{4,3,2,1,0:T(8,128)(2,1)S(1)}, u32[]{:S(2)}, u32[]{:S(2)}) collective-permute-start(bf16[4,2,3,16,128]{4,3,2,1,0:T(8,128)(2,1)S(1)} %get-tuple-element.24), channel_id=1, source_target_pairs={{0,1},{1,0},{2,3},{3,2},{4,5},{5,4},{6,7},{7,6},{8,9},{9,8},{10,11... | collective-permute-start | bytes 294920 | tf_op jit(solution)/shard_map/ppermute | solution.py:371
  34.3 0.5 collective-permute-start.5
  34.8 1.9 %green_pieces.1 = bf16[6,3,128,128]{3,2,1,0:T(8,128)(2,1)} custom-call(s32[1]{0:T(128)} %bitcast.1.side_ref, bf16[6,6,128,256]{3,2,1,0:T(8,128)(2,1)} %bitcast.17), custom_call_target="tpu_custom_call" | custom-call | tf_op jit(solution)/shard_map/green_pieces/pallas_call | solution.py:170
  36.7 1.6 %collective-permute-start.9 = (bf16[6,3,128,128]{3,2,1,0:T(8,128)(2,1)}, bf16[6,3,128,128]{3,2,1,0:T(8,128)(2,1)S(1)}, u32[]{:S(2)}, u32[]{:S(2)}) collective-permute-start(bf16[6,3,128,128]{3,2,1,0:T(8,128)(2,1)} %green_pieces.1), channel_id=1, source_target_pairs={{0,1},{1,0},{2,3},{3,2},{4,5},{5,4},{6,7},{7,6},{8,9},{9,8},{10,11... | collective-permute-start | bytes 1769480 | tf_op jit(solution)/shard_map/ppermute | solution.py:371
  38.2 1.5 %collective-permute-start.6 = (bf16[4,2,3,16,128]{4,3,2,1,0:T(8,128)(2,1)S(1)}, bf16[4,2,3,16,128]{4,3,2,1,0:T(8,128)(2,1)S(1)}, u32[]{:S(2)}, u32[]{:S(2)}) collective-permute-start(bf16[4,2,3,16,128]{4,3,2,1,0:T(8,128)(2,1)S(1)} %get-tuple-element.24), channel_id=1, source_target_pairs={{0,4},{2,6},{4,0},{6,2},{8,12},{10,14},{12,8},{14,10},{16,20},{18,... | collective-permute-start | bytes 294920 | tf_op jit(solution)/shard_map/ppermute | solution.py:368
  39.7 0.6 collective-permute-start.7
  40.3 2.6 %collective-permute-done.6 = bf16[4,2,3,16,128]{4,3,2,1,0:T(8,128)(2,1)S(1)} collective-permute-done((bf16[4,2,3,16,128]{4,3,2,1,0:T(8,128)(2,1)S(1)}, bf16[4,2,3,16,128]{4,3,2,1,0:T(8,128)(2,1)S(1)}, u32[]{:S(2)}, u32[]{:S(2)}) %collective-permute-start.6) | collective-permute-done | bytes 98336 | tf_op jit(solution)/shard_map/ppermute | solution.py:368
  42.9 1.5 %collective-permute-done.7 = bf16[4,2,3,16,128]{4,3,2,1,0:T(8,128)(2,1)S(1)} collective-permute-done((bf16[4,2,3,16,128]{4,3,2,1,0:T(8,128)(2,1)S(1)}, bf16[4,2,3,16,128]{4,3,2,1,0:T(8,128)(2,1)S(1)}, u32[]{:S(2)}, u32[]{:S(2)}) %collective-permute-start.7) | collective-permute-done | bytes 98336 | tf_op jit(solution)/shard_map/ppermute | solution.py:368
  44.4 0.1 collective-permute-start.8
  44.5 0.6 collective-permute-start.4
  45.0 1.4 %own_green.1.own_ref = bf16[6,6,128,128]{3,2,1,0:T(8,128)(2,1)S(1)} custom-call(s32[1]{0:T(128)} %bitcast.1.side_ref, bf16[6,6,128,256]{3,2,1,0:T(8,128)(2,1)} %bitcast.18), custom_call_target="tpu_custom_call" | custom-call | tf_op jit(solution)/shard_map/own_green/pallas_call | solution.py:199
  46.4 4.7 %collective-permute-done.5.other_ref = bf16[6,3,128,128]{3,2,1,0:T(8,128)(2,1)S(1)} collective-permute-done((bf16[6,3,128,128]{3,2,1,0:T(8,128)(2,1)}, bf16[6,3,128,128]{3,2,1,0:T(8,128)(2,1)S(1)}, u32[]{:S(2)}, u32[]{:S(2)}) %collective-permute-start.5) | collective-permute-done | bytes 589856 | tf_op jit(solution)/shard_map/ppermute | solution.py:371
  51.1 1.6 %shard_map.47 = (f32[256,384]{1,0:T(8,128)S(1)}, f32[256,384]{1,0:T(8,128)S(1)}, bf16[128,768]{1,0:T(8,128)(2,1)S(1)}) custom-call(bf16[2,4,2,3,16,128]{5,4,3,2,1,0:T(8,128)(2,1)S(1)} %pad_maximum_fusion.1.near_ref, bf16[2,4,2,3,16,128]{5,4,3,2,1,0:T(8,128)(2,1)} %collective-permute-done.8.core_ref, bf16[6,6,128,128]{3,2,1,0:T(8,128)(2,1)S(1)} %own_green.1.own_ref, ...), custom_call_target="tpu_custom_call" | custom-call | tf_op jit(solution)/shard_map/pallas_call | solution.py:269
  52.7 1.6 %shard_map.46 = (f32[256,384]{1,0:T(8,128)S(1)}, f32[256,384]{1,0:T(8,128)S(1)}, bf16[128,768]{1,0:T(8,128)(2,1)S(1)}) custom-call(bf16[2,4,2,3,16,128]{5,4,3,2,1,0:T(8,128)(2,1)S(1)} %pad_maximum_fusion.near_ref, bf16[2,4,2,3,16,128]{5,4,3,2,1,0:T(8,128)(2,1)} %collective-permute-done.4.core_ref, bf16[6,6,128,128]{3,2,1,0:T(8,128)(2,1)S(1)} %own_green.1.own_ref, ...), custom_call_target="tpu_custom_call" | custom-call | tf_op jit(solution)/shard_map/pallas_call | solution.py:269
  54.4 7.7 %collective-permute-done.9.other_ref = bf16[6,3,128,128]{3,2,1,0:T(8,128)(2,1)S(1)} collective-permute-done((bf16[6,3,128,128]{3,2,1,0:T(8,128)(2,1)}, bf16[6,3,128,128]{3,2,1,0:T(8,128)(2,1)S(1)}, u32[]{:S(2)}, u32[]{:S(2)}) %collective-permute-start.9) | collective-permute-done | bytes 589856 | tf_op jit(solution)/shard_map/ppermute | solution.py:371
  62.1 0.6 held_rest.1.full_ref
  62.7 0.8 %combine.1 = f32[2,128]{1,0:T(2,128)} custom-call(s32[1]{0:T(128)} %bitcast.me_ref, bf16[16,12,16,128]{3,2,1,0:T(8,128)(2,1)S(1)} %all-to-all-done.strain_ref, f32[2,256,768]{2,1,0:T(8,128)S(1)} %held_rest.1.full_ref), custom_call_target="tpu_custom_call" | custom-call | tf_op jit(solution)/shard_map/combine/pallas_call | solution.py:345
  (8 shorter events, 0.1 us)
Async XLA Ops:
  2.5 60.2 %all-to-all-start = ((bf16[16,12,16,128]{3,2,1,0:T(8,128)(2,1)}), bf16[16,12,16,128]{3,2,1,0:T(8,128)(2,1)S(1)}, u32[]{:S(2)}, u32[]{:S(2)}) async-start(bf16[16,12,16,128]{3,2,1,0:T(8,128)(2,1)} %get-tuple-element.14), calls=%async_computation | async-start | bytes 1572864 | tf_op jit(solution)/shard_map/all_to_all | solution.py:379
  9.9 14.4 %collective-permute-start = (bf16[2,3,16,128]{3,2,1,0:T(8,128)(2,1)S(1)}, bf16[2,3,16,128]{3,2,1,0:T(8,128)(2,1)S(1)}, u32[]{:S(2)}, u32[]{:S(2)}) collective-permute-start(bf16[2,3,16,128]{3,2,1,0:T(8,128)(2,1)S(1)} %get-tuple-element.15), channel_id=1, source_target_pairs={{0,8},{2,10},{4,12},{6,14},{8,0},{10,2},{12,4},{14,6},{16,24},{18,... | collective-permute-start | bytes 73736 | tf_op jit(solution)/shard_map/ppermute | solution.py:368
  11.9 20.8 %collective-permute-start.1 = (bf16[2,3,16,128]{3,2,1,0:T(8,128)(2,1)S(1)}, bf16[2,3,16,128]{3,2,1,0:T(8,128)(2,1)S(1)}, u32[]{:S(2)}, u32[]{:S(2)}) collective-permute-start(bf16[2,3,16,128]{3,2,1,0:T(8,128)(2,1)S(1)} %get-tuple-element.15), channel_id=1, source_target_pairs={{0,16},{2,18},{4,20},{6,22},{8,24},{10,26},{12,28},{14,30},{16,0},... | collective-permute-start | bytes 73736 | tf_op jit(solution)/shard_map/ppermute | solution.py:368
  14.2 18.4 %collective-permute-start.2 = (bf16[2,3,16,128]{3,2,1,0:T(8,128)(2,1)S(1)}, bf16[2,3,16,128]{3,2,1,0:T(8,128)(2,1)S(1)}, u32[]{:S(2)}, u32[]{:S(2)}) collective-permute-start(bf16[2,3,16,128]{3,2,1,0:T(8,128)(2,1)S(1)} %get-tuple-element.15), channel_id=1, source_target_pairs={{0,24},{2,26},{4,28},{6,30},{8,16},{10,18},{12,20},{14,22},{16,8},... | collective-permute-start | bytes 73736 | tf_op jit(solution)/shard_map/ppermute | solution.py:368
  32.7 7.0 %collective-permute-start.3 = (bf16[4,2,3,16,128]{4,3,2,1,0:T(8,128)(2,1)S(1)}, bf16[4,2,3,16,128]{4,3,2,1,0:T(8,128)(2,1)S(1)}, u32[]{:S(2)}, u32[]{:S(2)}) collective-permute-start(bf16[4,2,3,16,128]{4,3,2,1,0:T(8,128)(2,1)S(1)} %get-tuple-element.24), channel_id=1, source_target_pairs={{0,1},{1,0},{2,3},{3,2},{4,5},{5,4},{6,7},{7,6},{8,9},{9,8},{10,11... | collective-permute-start | bytes 294920 | tf_op jit(solution)/shard_map/ppermute | solution.py:371
  34.3 16.8 %collective-permute-start.5 = (bf16[6,3,128,128]{3,2,1,0:T(8,128)(2,1)}, bf16[6,3,128,128]{3,2,1,0:T(8,128)(2,1)S(1)}, u32[]{:S(2)}, u32[]{:S(2)}) collective-permute-start(bf16[6,3,128,128]{3,2,1,0:T(8,128)(2,1)} %get-tuple-element.16), channel_id=1, source_target_pairs={{0,1},{1,0},{2,3},{3,2},{4,5},{5,4},{6,7},{7,6},{8,9},{9,8},{10,11... | collective-permute-start | bytes 1769480 | tf_op jit(solution)/shard_map/ppermute | solution.py:371
  36.7 25.4 %collective-permute-start.9 = (bf16[6,3,128,128]{3,2,1,0:T(8,128)(2,1)}, bf16[6,3,128,128]{3,2,1,0:T(8,128)(2,1)S(1)}, u32[]{:S(2)}, u32[]{:S(2)}) collective-permute-start(bf16[6,3,128,128]{3,2,1,0:T(8,128)(2,1)} %green_pieces.1), channel_id=1, source_target_pairs={{0,1},{1,0},{2,3},{3,2},{4,5},{5,4},{6,7},{7,6},{8,9},{9,8},{10,11... | collective-permute-start | bytes 1769480 | tf_op jit(solution)/shard_map/ppermute | solution.py:371
  38.2 4.6 %collective-permute-start.6 = (bf16[4,2,3,16,128]{4,3,2,1,0:T(8,128)(2,1)S(1)}, bf16[4,2,3,16,128]{4,3,2,1,0:T(8,128)(2,1)S(1)}, u32[]{:S(2)}, u32[]{:S(2)}) collective-permute-start(bf16[4,2,3,16,128]{4,3,2,1,0:T(8,128)(2,1)S(1)} %get-tuple-element.24), channel_id=1, source_target_pairs={{0,4},{2,6},{4,0},{6,2},{8,12},{10,14},{12,8},{14,10},{16,20},{18,... | collective-permute-start | bytes 294920 | tf_op jit(solution)/shard_map/ppermute | solution.py:368
  39.7 4.6 %collective-permute-start.7 = (bf16[4,2,3,16,128]{4,3,2,1,0:T(8,128)(2,1)S(1)}, bf16[4,2,3,16,128]{4,3,2,1,0:T(8,128)(2,1)S(1)}, u32[]{:S(2)}, u32[]{:S(2)}) collective-permute-start(bf16[4,2,3,16,128]{4,3,2,1,0:T(8,128)(2,1)S(1)} %collective-permute-done.3), channel_id=1, source_target_pairs={{0,4},{2,6},{4,0},{6,2},{8,12},{10,14},{12,8},{14,10},{16,20},{18,... | collective-permute-start | bytes 294920 | tf_op jit(solution)/shard_map/ppermute | solution.py:368
  44.4 2.1 %collective-permute-start.8 = (bf16[2,4,2,3,16,128]{5,4,3,2,1,0:T(8,128)(2,1)S(1)}, bf16[2,4,2,3,16,128]{5,4,3,2,1,0:T(8,128)(2,1)}, u32[]{:S(2)}, u32[]{:S(2)}) collective-permute-start(bf16[2,4,2,3,16,128]{5,4,3,2,1,0:T(8,128)(2,1)S(1)} %pad_maximum_fusion.1.near_ref), channel_id=1, source_target_pairs={{0,2},{2,0},{4,6},{6,4},{8,10},{10,8},{12,14},{14,12},{16,18},{18,... | collective-permute-start | bytes 589832 | tf_op jit(solution)/shard_map/ppermute | solution.py:368
  44.5 8.3 %collective-permute-start.4 = (bf16[2,4,2,3,16,128]{5,4,3,2,1,0:T(8,128)(2,1)S(1)}, bf16[2,4,2,3,16,128]{5,4,3,2,1,0:T(8,128)(2,1)}, u32[]{:S(2)}, u32[]{:S(2)}) collective-permute-start(bf16[2,4,2,3,16,128]{5,4,3,2,1,0:T(8,128)(2,1)S(1)} %pad_maximum_fusion.near_ref), channel_id=1, source_target_pairs={{0,2},{2,0},{4,6},{6,4},{8,10},{10,8},{12,14},{14,12},{16,18},{18,... | collective-permute-start | bytes 589832 | tf_op jit(solution)/shard_map/ppermute | solution.py:368
